TPU v7x, 512 devices: a whole 4x4x16 slice. The times are simulated.
512 devices in a mesh: member: 32 (over z, x_lo), tensor: 4 (over x_hi, core), answer: 4 (over y).
Axes of the slice: x: 4 (x_hi: 2, x_lo: 2; x = x_hi * 2 + x_lo), y: 4, z: 16, core: 2. Of those that a mesh axis runs over, the one named last changes fastest.
Arguments:
- master: float32 [5120, 13824], P('member', ('tensor', 'answer')), may hold values from -6 to 6
- left_noise: bfloat16 [4096, 5120], P(('member', 'answer')), may hold values from -5 to 5
- right_noise: bfloat16 [4096, 13824], P(('member', 'answer'), 'tensor'), may hold values from -5 to 5
- returns: float32 [4096, 512], P('member', 'answer'), may hold values from -12 to 12
Outputs:
- new_master: float32 [5120, 13824], P('member', ('tensor', 'answer'))
- rollout: bfloat16 [5120, 13824], P(('member', 'answer'), 'tensor')
All inputs are finite; a program needn't handle non-finite values.
Results may differ from a plain program's by a relative error of at most 0.01.
Values may be sent and summed in bfloat16 or wider, within the bound.
No kernel may reach another device: no remote copies, remote signals or barrier semaphores. Data moves between devices by JAX's collectives and lax.ppermute only.
A program may use at most 64 MiB of HBM per device.

v0:
```python
import functools

import jax
import jax.numpy as jnp
from jax import lax
from jax.sharding import Mesh
from jax.sharding import PartitionSpec as P

MEMBER = ("member_0", "member_1")
MEMBER_ANSWER = ("member_0", "member_1", "answer")


def by_axis(value, axes):
    return functools.reduce(lax.psum, axes, value)


def gather_axes(value, axes, dim):
    out = value
    for number in range(len(axes) - 1, -1, -1):
        out = lax.all_gather(out, axes[number], axis=dim, tiled=True)
    return out


def split_up(value, dim, count):
    before, after = (value.shape[:dim], value.shape[dim + 1 :])
    return jnp.moveaxis(value.reshape(*before, count, -1, *after), dim, 0)


def sent_and_summed(value, axis, dim):
    count = lax.axis_size(axis)
    blocks = lax.all_to_all(split_up(value, dim, count), axis, 0, 0, tiled=True)
    return jnp.sum(blocks.astype(jnp.float32), axis=0)


def contract(left_tile, accum, pieces):
    right_cols, weights = pieces
    weighted = left_tile.astype(jnp.float32) * weights[:, None]
    return accum + lax.dot_general(
        weighted,
        right_cols.astype(jnp.float32),
        (((0,), (0,)), ((), ())),
        precision=lax.Precision.HIGHEST,
    )


def body(master, left_noise, right_noise, returns):
    member_count = lax.axis_size(MEMBER)
    answer_place = lax.axis_index("answer")
    partial_value = jnp.sum(returns, axis=1)
    block_len = partial_value.shape[0]
    population = block_len * member_count
    scores = lax.psum(partial_value, "answer")
    score_sum, square_sum = (
        by_axis(jnp.sum(scores), MEMBER),
        by_axis(jnp.sum(scores * scores), MEMBER),
    )
    average = score_sum / population
    variance = square_sum / population - average * average
    fitness = (scores - average) / jnp.sqrt(variance + 1e-05)
    tile_rows = master.shape[0]
    left_tile = lax.all_to_all(left_noise, MEMBER, split_axis=1, concat_axis=0, tiled=True)
    member_share = right_noise.shape[0]
    fitness_share = lax.dynamic_slice_in_dim(fitness, answer_place * member_share, member_share, 0)
    initial = jnp.zeros((tile_rows, right_noise.shape[1]), jnp.float32)
    partial_update = contract(
        left_tile,
        initial,
        (
            gather_axes(right_noise, MEMBER, 0),
            gather_axes(fitness_share.astype(jnp.bfloat16), MEMBER, 0).astype(jnp.float32),
        ),
    )
    update = sent_and_summed(partial_update.astype(jnp.bfloat16), "answer", 1)
    new_master = master + update / jnp.sqrt(jnp.float32(population))
    rollout = lax.all_to_all(
        new_master.astype(jnp.bfloat16), "answer", split_axis=0, concat_axis=1, tiled=True
    )
    return (new_master, rollout)


def solution(mesh):
    finer = Mesh(
        mesh.devices.reshape(16, 2, mesh.shape["tensor"], mesh.shape["answer"]),
        ("member_0", "member_1", "tensor", "answer"),
    )
    placed = (
        P(MEMBER, ("tensor", "answer")),
        P(MEMBER_ANSWER, None),
        P(MEMBER_ANSWER, "tensor"),
        P(MEMBER, "answer"),
    )
    return jax.shard_map(
        body,
        mesh=finer,
        in_specs=placed,
        out_specs=(P(MEMBER, ("tensor", "answer")), P(MEMBER_ANSWER, "tensor")),
        check_vma=False,
    )
```

profile of v0, /device:TPU:6, one launch (start us, length us, event | category | flops | bytes accessed | tf_op | source)
XLA Modules:
  0.0 180.7 jit_solution(4885161245045495839)
XLA Ops:
  7.2 8.9 %all_gather.14 = bf16[64,3456]{1,0:T(8,128)(2,1)} all-gather(bf16[32,3456]{1,0:T(8,128)(2,1)} %param.6), channel_id=1, replica_groups=mesh['member_0'=16,'member_1'=2,'tensor'=4,'answer'=4] {'member_1'}, dimensions={0}, use_global_device_ids=true | all-gather | bytes 663552 | tf_op jit(solution)/shard_map/all_gather | solution.py:20
  16.1 1.6 all_to_all.27
  17.7 1.1 copy.11
  18.8 16.7 %all-to-all-start = ((bf16[32,32,160]{2,0,1:T(8,128)(2,1)}), bf16[32,32,160]{2,0,1:T(8,128)(2,1)S(1)}, u32[]{:S(2)}, u32[]{:S(2)}) async-start(bf16[32,32,160]{2,0,1:T(8,128)(2,1)} %copy.11), calls=%async_computation | async-start | bytes 1048576 | tf_op jit(solution)/shard_map/all_to_all | solution.py:61
  35.6 10.7 %psum.35 = f32[128]{0:T(128)S(1)} all-reduce(f32[128]{0:T(128)S(1)} %reduce_sum.36), channel_id=1, replica_groups=mesh['member_0'=16,'member_1'=2,'tensor'=4,'answer'=4] {'answer'}, use_global_device_ids=true, to_apply=%region_1.0 | all-reduce | flops 128 | bytes 1024 | tf_op jit(solution)/shard_map/psum | solution.py:52
  46.4 0.6 fusion
  47.0 42.6 %all-reduce.2 = (f32[]{:T(128)}, f32[]{:T(128)}) all-reduce(f32[]{:T(128)} %get-tuple-element.3, f32[]{:T(128)} %get-tuple-element.2), channel_id=1, replica_groups=mesh['member_0'=16,'member_1'=2,'tensor'=4,'answer'=4] {'member_0'}, use_global_device_ids=true, to_apply=%region_6.0 | all-reduce | flops 2 | bytes 16 | tf_op jit(solution)/shard_map/psum | solution.py:14
  89.6 5.6 %all-reduce.3 = (f32[]{:T(128)}, f32[]{:T(128)}) all-reduce(f32[]{:T(128)} %get-tuple-element.4, f32[]{:T(128)} %get-tuple-element.5), channel_id=1, replica_groups=mesh['member_0'=16,'member_1'=2,'tensor'=4,'answer'=4] {'member_1'}, use_global_device_ids=true, to_apply=%region_7.0 | all-reduce | flops 2 | bytes 16 | tf_op jit(solution)/shard_map/psum | solution.py:14
  95.2 1.3 dynamic-slice.1
  96.5 1.2 dynamic-slice
  101.7 0.2 dynamic-update-slice
  101.9 4.9 %all-reduce = bf16[64]{0:T(256)(128)(2,1)S(1)} all-reduce(bf16[64]{0:T(256)(128)(2,1)S(1)} %dynamic-update-slice), channel_id=1, replica_groups=mesh['member_0'=16,'member_1'=2,'tensor'=4,'answer'=4] {'member_1'}, use_global_device_ids=true, to_apply=%add | all-reduce | flops 64 | bytes 256
  106.8 0.2 dynamic-update-slice.1
  107.0 27.7 %all-reduce.1 = bf16[1024]{0:T(1024)(128)(2,1)S(1)} all-reduce(bf16[1024]{0:T(1024)(128)(2,1)S(1)} %dynamic-update-slice.1), channel_id=1, replica_groups=mesh['member_0'=16,'member_1'=2,'tensor'=4,'answer'=4] {'member_0'}, use_global_device_ids=true, to_apply=%add.1 | all-reduce | flops 1024 | bytes 4096
  134.7 0.2 bitcast_multiply_fusion
  134.9 6.8 %convolution_convert_fusion = bf16[160,3456]{1,0:T(8,128)(2,1)S(1)} fusion(f32[1024,160]{1,0:T(8,128)S(1)} %bitcast_multiply_fusion, bf16[1024,3456]{1,0:T(8,128)(2,1)} %all-gather.2.cloned.1.call-done), kind=kOutput, calls=%fused_computation | convolution fusion | flops 6795325440 | bytes 8839168 | tf_op jit(solution)/shard_map/dot_general | solution.py:38
  141.7 0.9 reshape.16
  142.7 0.1 copy.15
  142.8 19.7 %all_to_all.37 = bf16[4,160,864]{2,1,0:T(8,128)(2,1)S(1)} all-to-all(bf16[4,160,864]{2,1,0:T(8,128)(2,1)S(1)} %bitcast.13), channel_id=1, replica_groups=mesh['member_0'=16,'member_1'=2,'tensor'=4,'answer'=4] {'answer'}, dimensions={0} | all-to-all | bytes 2211840 | tf_op jit(solution)/shard_map/all_to_all | solution.py:31
  162.5 0.2 convert_reduce_fusion
  162.7 0.9 fusion.1
  163.6 9.2 %all_to_all.38 = bf16[4,40,864]{2,1,0:T(8,128)(2,1)S(1)} all-to-all(bf16[4,40,864]{2,1,0:T(8,128)(2,1)S(1)} %bitcast.15), channel_id=1, replica_groups=mesh['member_0'=16,'member_1'=2,'tensor'=4,'answer'=4] {'answer'}, dimensions={0} | all-to-all | bytes 552960 | tf_op jit(solution)/shard_map/all_to_all | solution.py:75
  172.7 0.1 copy.13
  172.9 0.9 all_to_all.33
  (14 shorter events, 0.3 us)
Async XLA Ops:
  7.2 28.4 %copy-start.1 = (f32[128,128]{1,0:T(8,128)S(1)}, f32[128,128]{1,0:T(8,128)}, u32[]{:S(2)}) copy-start(f32[128,128]{1,0:T(8,128)} %param.7) | copy-start | bytes 196612
  7.2 127.7 %all-gather.2.cloned.1.call-start = ((), (), s32[]{:S(2)}) async-start(), calls=%async_computation.3 | async-start | bytes 7520256 | tf_op jit(solution)/shard_map/all_gather | solution.py:20
  18.8 115.9 %all-to-all-start = ((bf16[32,32,160]{2,0,1:T(8,128)(2,1)}), bf16[32,32,160]{2,0,1:T(8,128)(2,1)S(1)}, u32[]{:S(2)}, u32[]{:S(2)}) async-start(bf16[32,32,160]{2,0,1:T(8,128)(2,1)} %copy.11), calls=%async_computation | async-start | bytes 1048576 | tf_op jit(solution)/shard_map/all_to_all | solution.py:61
  142.8 19.9 %copy-start = (f32[160,864]{1,0:T(8,128)S(1)}, f32[160,864]{1,0:T(8,128)}, u32[]{:S(2)}) copy-start(f32[160,864]{1,0:T(8,128)} %param.4) | copy-start | bytes 1658884
Sparse Core Ops, SparseCore 0:
  16.2 117.5 all-gather.1
where the time goes:
time: 181 us
  blocking collectives  129 us (71%)
  between operations  18 us (10%)
  starting transfers between devices  16.7 us (9%)
  local copies, waits for them, and re-layouts  7.87 us (4%)
  matrix products  6.79 us (4%)
  other arithmetic  2.02 us (1%)
    psum x2, blocking collectives, by_axis(): return functools.reduce(lax.psum, axes, value)  48.2 us
    unnamed x2, blocking collectives  32.6 us
    all_to_all x1, blocking collectives, sent_and_summed(): blocks = lax.all_to_all(split_up(value, dim, count), axis, 0, 0, tiled=True)  19.7 us
    all_to_all x1, starting transfers between devices, body(): lax.all_to_all(left_noise, MEMBER, split_axis=1, concat_axis=0, tiled=True)  16.7 us
    psum x1, blocking collectives, body(): scores = lax.psum(partial_value, 'answer')  10.7 us
    all_to_all x1, blocking collectives, body(): lax.all_to_all(new_master.astype(jnp.bfloat16), 'answer', split_axis=0, c...  9.15 us
    all_gather x1, blocking collectives, gather_axes(): out = lax.all_gather(out, axes[number], axis=dim, tiled=True)  8.86 us
    dot_general x1, matrix products, contract(): lax.dot_general(weighted, right_cols.astype(jnp.float32), (((0,), (0,)),...  6.79 us
  transfers between devices with their start and end apart: 2, of which 0 were waited for; matrix products, arithmetic and copies ran while one was open for 3% of the time, Pallas kernels for 0%

commit v1 on v0

v1 whole, which is shorter than its diff:
```python
import jax
import jax.numpy as jnp
from jax import lax
from jax.sharding import Mesh
from jax.sharding import PartitionSpec as P

MEMBER = ("depth", "near")
MEMBER_ANSWER = ("depth", "near", "answer")


def spread(value, axes):
    count = lax.axis_size(axes)
    copies = jnp.broadcast_to(value[None], (count, *value.shape))
    return lax.all_to_all(copies, axes, 0, 0, tiled=True)


def body(master, left_noise, right_noise, returns):
    depth, near, answers = (lax.axis_size(a) for a in ("depth", "near", "answer"))
    share = right_noise.shape[0]
    tile_rows, tile_cols = master.shape
    population = share * depth * near * answers
    near_place = lax.axis_index("near")

    right_part = lax.all_to_all(right_noise, "answer", split_axis=1, concat_axis=0, tiled=True)
    right_cols = lax.all_gather(right_part, "depth", axis=0, tiled=True)

    left_noise, returns, _ = lax.optimization_barrier((left_noise, returns, right_part))
    left_part = lax.all_to_all(left_noise, "depth", split_axis=1, concat_axis=0, tiled=True)
    scores = lax.psum(jnp.sum(returns, axis=1), "answer")
    all_scores = spread(scores, MEMBER)
    average = jnp.sum(all_scores) / population
    variance = jnp.sum(all_scores * all_scores) / population - average * average
    fitness = (all_scores - average) / jnp.sqrt(variance + 1e-05)
    fitness = fitness.reshape(depth, near, answers, share)
    fitness = lax.dynamic_index_in_dim(fitness, near_place, 1, keepdims=False)

    left_rows = spread(left_part, "answer").reshape(answers, depth, share, near * tile_rows)
    weighted = left_rows.transpose(1, 0, 2, 3).astype(jnp.float32) * fitness[..., None]
    weighted = weighted.astype(jnp.bfloat16).reshape(-1, near * tile_rows)
    partial_update = lax.dot_general(
        weighted, right_cols, (((0,), (0,)), ((), ())), preferred_element_type=jnp.float32
    )
    partial_update = partial_update.reshape(near, tile_rows, tile_cols)
    kept = lax.dynamic_index_in_dim(partial_update, near_place, 0, keepdims=False)
    sent = lax.dynamic_index_in_dim(partial_update, 1 - near_place, 0, keepdims=False)
    received = lax.ppermute(sent.astype(jnp.bfloat16), "near", [(0, 1), (1, 0)])
    update = kept + received.astype(jnp.float32)
    new_master = master + update / jnp.sqrt(jnp.float32(population))
    rollout = lax.all_to_all(
        new_master.astype(jnp.bfloat16), "answer", split_axis=0, concat_axis=1, tiled=True
    )
    return (new_master, rollout)


def solution(mesh):
    finer = Mesh(
        mesh.devices.reshape(-1, 2, mesh.shape["tensor"], mesh.shape["answer"]),
        ("depth", "near", "tensor", "answer"),
    )
    placed = (
        P(MEMBER, ("tensor", "answer")),
        P(MEMBER_ANSWER, None),
        P(MEMBER_ANSWER, "tensor"),
        P(MEMBER, "answer"),
    )
    return jax.shard_map(
        body,
        mesh=finer,
        in_specs=placed,
        out_specs=(P(MEMBER, ("tensor", "answer")), P(MEMBER_ANSWER, "tensor")),
        check_vma=False,
    )
```

time: 181 us -> 155 us (0.86)
  blocking collectives: 129 us -> 28.8 us
  waiting for transfers between devices: 0.04 us -> 64.1 us
  starting transfers between devices: 16.7 us -> 30.1 us
  matrix products: 6.79 us -> 3.61 us
    psum x3 -> x1, blocking collectives: 58.9 us -> 8.9 us  [body(): scores = lax.psum(jnp.sum(returns, axis=1), 'answer')]
    all_to_all x1 -> x3, waiting for transfers between devices: 0.01 us -> 38.7 us  [the longest x2 22.9 us: spread(): return lax.all_to_all(copies, axes, 0, 0, tiled=True)]
    unnamed x2 -> x0, blocking collectives: 32.6 us -> none
    all_gather x1, waiting for transfers between devices: 0.02 us -> 19.6 us  [body(): right_cols = lax.all_gather(right_part, 'depth', axis=0, tiled=True)]
    all_to_all x1 -> x3, starting transfers between devices: 16.7 us -> 27.3 us  [the longest x1 15.2 us: body(): lax.all_to_all(left_noise, 'depth', split_axis=1, concat_axis=0, tiled=True)]
    all_to_all x1, blocking collectives: 19.7 us -> 10.8 us  [body(): lax.all_to_all(right_noise, 'answer', split_axis=1, concat_axis=0, tiled=...]
    all_gather x1 -> x0, blocking collectives: 8.86 us -> none  [gather_axes(): out = lax.all_gather(out, axes[number], axis=dim, tiled=True)]
    ppermute x0 -> x1, waiting for transfers between devices: none -> 5.81 us  [body(): received = lax.ppermute(sent.astype(jnp.bfloat16), 'near', [(0, 1), (1, 0)])]
  transfers between devices with their start and end apart: 2 -> 5, of which waited for: 0 -> 5; matrix products, arithmetic and copies ran while one was open for 3% -> 4% of each run, Pallas kernels for 0% -> 0%
where the time goes in v1:
time: 155 us; the launch traced here: 154 us
  waiting for transfers between devices  64.1 us (41%)
  starting transfers between devices  30.1 us (19%)
  blocking collectives  28.8 us (19%)
  between operations  16.9 us (11%)
  local copies, waits for them, and re-layouts  8.18 us (5%)
  matrix products  3.61 us (2%)
  other arithmetic  2.12 us (1%)
    all_to_all x2, waiting for transfers between devices, spread(): return lax.all_to_all(copies, axes, 0, 0, tiled=True)  22.9 us
    all_gather x1, waiting for transfers between devices, body(): right_cols = lax.all_gather(right_part, 'depth', axis=0, tiled=True)  19.6 us
    all_to_all x1, waiting for transfers between devices, body(): lax.all_to_all(left_noise, 'depth', split_axis=1, concat_axis=0, tiled=True)  15.8 us
    all_to_all x1, starting transfers between devices, body(): lax.all_to_all(left_noise, 'depth', split_axis=1, concat_axis=0, tiled=True)  15.2 us
    all_to_all x2, starting transfers between devices, spread(): return lax.all_to_all(copies, axes, 0, 0, tiled=True)  12.1 us
    all_to_all x1, blocking collectives, body(): lax.all_to_all(right_noise, 'answer', split_axis=1, concat_axis=0, tiled=...  10.8 us
    all_to_all x1, blocking collectives, body(): lax.all_to_all(new_master.astype(jnp.bfloat16), 'answer', split_axis=0, c...  9.15 us
    psum x1, blocking collectives, body(): scores = lax.psum(jnp.sum(returns, axis=1), 'answer')  8.9 us
  transfers between devices with their start and end apart: 5, of which 5 were waited for; matrix products, arithmetic and copies ran while one was open for 4% of the time, Pallas kernels for 0%

profile of v1, /device:TPU:6, one launch (start us, length us, event | category | flops | bytes accessed | tf_op | source)
XLA Modules:
  0.0 153.8 jit_solution(13344871915087925581)
XLA Ops:
  7.2 1.2 all_to_all.47
  8.4 10.8 %all_to_all.65 = bf16[32,4,864]{2,0,1:T(8,128)(2,1)S(1)} all-to-all(bf16[32,4,864]{2,0,1:T(8,128)(2,1)S(1)} %copy.21), channel_id=1, replica_groups=mesh['depth'=16,'near'=2,'tensor'=4,'answer'=4] {'answer'}, dimensions={1} | all-to-all | bytes 442368 | tf_op jit(solution)/shard_map/all_to_all | solution.py:24
  19.2 0.8 copy.28
  20.4 0.8 copy.22
  21.2 15.2 %all-to-all-start.1 = ((bf16[32,16,320]{2,0,1:T(8,128)(2,1)}), bf16[32,16,320]{2,0,1:T(8,128)(2,1)S(1)}, u32[]{:S(2)}, u32[]{:S(2)}) async-start(bf16[32,16,320]{2,0,1:T(8,128)(2,1)} %copy.22), calls=%async_computation.1 | async-start | bytes 786432 | tf_op jit(solution)/shard_map/all_to_all | solution.py:28
  36.5 8.9 %psum.7 = f32[128]{0:T(128)S(1)} all-reduce(f32[128]{0:T(128)S(1)} %reduce_sum.27), channel_id=1, replica_groups=mesh['depth'=16,'near'=2,'tensor'=4,'answer'=4] {'answer'}, use_global_device_ids=true, to_apply=%region_1.0 | all-reduce | flops 128 | bytes 1024 | tf_op jit(solution)/shard_map/psum | solution.py:29
  45.4 15.8 %all-to-all-done.1 = bf16[32,16,320]{2,0,1:T(8,128)(2,1)S(1)} async-done(((bf16[32,16,320]{2,0,1:T(8,128)(2,1)}), bf16[32,16,320]{2,0,1:T(8,128)(2,1)S(1)}, u32[]{:S(2)}, u32[]{:S(2)}) %all-to-all-start.1) | async-done | bytes 327712 | tf_op jit(solution)/shard_map/all_to_all | solution.py:28
  61.3 0.6 broadcast_in_dim.8
  61.9 8.6 %all-to-all-start.3 = ((f32[32,1,128]{2,1,0:T(1,128)}), f32[32,1,128]{2,1,0:T(1,128)S(1)}, u32[]{:S(2)}, u32[]{:S(2)}) async-start(f32[32,1,128]{2,1,0:T(1,128)} %broadcast_in_dim.8), calls=%async_computation.3 | async-start | bytes 32768 | tf_op jit(solution)/shard_map/all_to_all | solution.py:14
  70.6 11.8 %all-to-all-done.3 = f32[32,1,128]{2,1,0:T(1,128)S(1)} async-done(((f32[32,1,128]{2,1,0:T(1,128)}), f32[32,1,128]{2,1,0:T(1,128)S(1)}, u32[]{:S(2)}, u32[]{:S(2)}) %all-to-all-start.3) | async-done | bytes 16416 | tf_op jit(solution)/shard_map/all_to_all | solution.py:14
  82.5 1.2 broadcast_in_dim.7
  83.7 3.5 %all-to-all-start.2 = ((bf16[4,512,320]{1,2,0:T(8,128)(2,1)}), bf16[4,512,320]{1,2,0:T(8,128)(2,1)S(1)}, u32[]{:S(2)}, u32[]{:S(2)}) async-start(bf16[4,512,320]{1,2,0:T(8,128)(2,1)} %broadcast_in_dim.7), calls=%async_computation.2 | async-start | bytes 2621440 | tf_op jit(solution)/shard_map/all_to_all | solution.py:14
  87.2 0.7 fusion.7
  90.8 11.0 %all-to-all-done.2 = bf16[4,512,320]{1,2,0:T(8,128)(2,1)S(1)} async-done(((bf16[4,512,320]{1,2,0:T(8,128)(2,1)}), bf16[4,512,320]{1,2,0:T(8,128)(2,1)S(1)}, u32[]{:S(2)}, u32[]{:S(2)}) %all-to-all-start.2) | async-done | bytes 1310752 | tf_op jit(solution)/shard_map/all_to_all | solution.py:14
  101.8 0.8 copy.24
  102.7 0.3 fusion.3
  103.3 0.7 copy.27
  104.0 19.6 %all-gather.2.cloned.1.call-done = bf16[2048,864]{0,1:T(8,128)(2,1)} async-done(((bf16[128,864]{0,1:T(8,128)(2,1)}), bf16[2048,864]{0,1:T(8,128)(2,1)}) %all-gather.2.cloned.1.call-update) | async-done | bytes 3538960 | tf_op jit(solution)/shard_map/all_gather | solution.py:25
  123.6 3.6 %fusion = f32[2,160,864]{2,1,0:T(8,128)S(1)} fusion(bf16[2,160,2048]{2,1,0:T(8,128)(2,1)S(1)} %bitcast.39, bf16[2048,864]{0,1:T(8,128)(2,1)} %all-gather.2.cloned.1.call-done), kind=kOutput, calls=%fused_computation | convolution fusion | flops 1132462080 | bytes 5955584 | tf_op jit(solution)/shard_map/dot_general | solution.py:40
  127.3 2.7 %collective-permute-start = (bf16[160,864]{1,0:T(8,128)(2,1)S(1)}, bf16[160,864]{1,0:T(8,128)(2,1)S(1)}, u32[]{:S(2)}, u32[]{:S(2)}) collective-permute-start(bf16[160,864]{1,0:T(8,128)(2,1)S(1)} %fusion.6), channel_id=1, source_target_pairs={{0,16},{16,0},{1,17},{17,1},{2,18},{18,2},{3,19},{19,3},{4,20},{20... | collective-permute-start | bytes 829448 | tf_op jit(solution)/shard_map/ppermute | solution.py:46
  130.0 5.8 %collective-permute-done = bf16[160,864]{1,0:T(8,128)(2,1)S(1)} collective-permute-done((bf16[160,864]{1,0:T(8,128)(2,1)S(1)}, bf16[160,864]{1,0:T(8,128)(2,1)S(1)}, u32[]{:S(2)}, u32[]{:S(2)}) %collective-permute-start) | collective-permute-done | bytes 276512 | tf_op jit(solution)/shard_map/ppermute | solution.py:46
  135.8 0.9 fusion.8
  136.7 9.2 %all_to_all.66 = bf16[4,40,864]{2,1,0:T(8,128)(2,1)S(1)} all-to-all(bf16[4,40,864]{2,1,0:T(8,128)(2,1)S(1)} %bitcast.40), channel_id=1, replica_groups=mesh['depth'=16,'near'=2,'tensor'=4,'answer'=4] {'answer'}, dimensions={0} | all-to-all | bytes 552960 | tf_op jit(solution)/shard_map/all_to_all | solution.py:49
  146.0 0.9 all_to_all.59
  (19 shorter events, 1.3 us)
Async XLA Ops:
  7.2 12.9 %copy-start.1 = (bf16[32,5120]{1,0:T(8,128)(2,1)S(1)}, bf16[32,5120]{1,0:T(8,128)(2,1)}, u32[]{:S(2)}) copy-start(bf16[32,5120]{1,0:T(8,128)(2,1)} %param.5) | copy-start | bytes 983044
  7.2 116.4 %all-gather.2.cloned.1.call-start = ((), (), s32[]{:S(2)}) async-start(), calls=%async_computation.5 | async-start | bytes 3760128 | tf_op jit(solution)/shard_map/all_gather | solution.py:25
  19.2 17.2 %copy-start.2 = (f32[128,128]{1,0:T(8,128)S(1)}, f32[128,128]{1,0:T(8,128)}, u32[]{:S(2)}) copy-start(f32[128,128]{1,0:T(8,128)} %param.7) | copy-start | bytes 196612
  21.2 40.1 %all-to-all-start.1 = ((bf16[32,16,320]{2,0,1:T(8,128)(2,1)}), bf16[32,16,320]{2,0,1:T(8,128)(2,1)S(1)}, u32[]{:S(2)}, u32[]{:S(2)}) async-start(bf16[32,16,320]{2,0,1:T(8,128)(2,1)} %copy.22), calls=%async_computation.1 | async-start | bytes 786432 | tf_op jit(solution)/shard_map/all_to_all | solution.py:28
  61.9 20.6 %all-to-all-start.3 = ((f32[32,1,128]{2,1,0:T(1,128)}), f32[32,1,128]{2,1,0:T(1,128)S(1)}, u32[]{:S(2)}, u32[]{:S(2)}) async-start(f32[32,1,128]{2,1,0:T(1,128)} %broadcast_in_dim.8), calls=%async_computation.3 | async-start | bytes 32768 | tf_op jit(solution)/shard_map/all_to_all | solution.py:14
  83.7 18.2 %all-to-all-start.2 = ((bf16[4,512,320]{1,2,0:T(8,128)(2,1)}), bf16[4,512,320]{1,2,0:T(8,128)(2,1)S(1)}, u32[]{:S(2)}, u32[]{:S(2)}) async-start(bf16[4,512,320]{1,2,0:T(8,128)(2,1)} %broadcast_in_dim.7), calls=%async_computation.2 | async-start | bytes 2621440 | tf_op jit(solution)/shard_map/all_to_all | solution.py:14
  123.6 12.2 %copy-start = (f32[160,864]{1,0:T(8,128)S(1)}, f32[160,864]{1,0:T(8,128)}, u32[]{:S(2)}) copy-start(f32[160,864]{1,0:T(8,128)} %param.4) | copy-start | bytes 1658884
  127.3 8.5 %collective-permute-start = (bf16[160,864]{1,0:T(8,128)(2,1)S(1)}, bf16[160,864]{1,0:T(8,128)(2,1)S(1)}, u32[]{:S(2)}, u32[]{:S(2)}) collective-permute-start(bf16[160,864]{1,0:T(8,128)(2,1)S(1)} %fusion.6), channel_id=1, source_target_pairs={{0,16},{16,0},{1,17},{17,1},{2,18},{18,2},{3,19},{19,3},{4,20},{20... | collective-permute-start | bytes 829448 | tf_op jit(solution)/shard_map/ppermute | solution.py:46
Sparse Core Ops, SparseCore 0:
  20.2 103.3 all-gather.1

commit v2 on v1

v2 whole, which is shorter than its diff:
```python
import math

import jax
import jax.numpy as jnp
from jax import lax
from jax.sharding import Mesh
from jax.sharding import PartitionSpec as P

MEMBER = ("depth", "near")
TENSOR = ("far", "core")
ANSWER = "answer"
RIGHT_SCALE = 2.0**13
PIECE = 2.0**11


def spread(value, axes):
    copies = jnp.broadcast_to(value[None], (lax.axis_size(axes), *value.shape))
    return lax.all_to_all(copies, axes, 0, 0, tiled=True)


def pieces(value):
    high = lax.reduce_precision(value, 5, 10)
    rest = (value - high) * PIECE
    middle = lax.reduce_precision(rest, 5, 10)
    low = (rest - middle) * PIECE
    return jnp.stack([high, middle, low]).astype(jnp.float16)


def joined(parts):
    high, middle, low = (parts[i].astype(jnp.float32) for i in range(3))
    return high + (middle + low / PIECE) / PIECE


def body(master, left_noise, right_noise, returns):
    depth, near, cores, answers = (lax.axis_size(a) for a in ("depth", "near", "core", ANSWER))
    share = right_noise.shape[0]
    tile_rows, tile_cols = master.shape
    block = share * answers
    population = block * depth * near
    near_place = lax.axis_index("near")
    score_scale = 2.0 ** math.floor(math.log2(32768.0 / (12.0 * answers * returns.shape[1])))

    half = left_noise.reshape(share, depth, cores, -1)
    half = lax.dynamic_index_in_dim(half, lax.axis_index("core"), 2, keepdims=False)
    half = lax.all_to_all(half.transpose(1, 0, 2), "depth", 0, 0, tiled=True)
    left_rows = spread(half, ("core", ANSWER)).reshape(cores, answers, depth, share, -1)

    partial_scores = spread(jnp.sum(returns, axis=1), ("near", ANSWER))
    scores = jnp.sum(partial_scores.reshape(near, answers, block), axis=1)

    right_part = lax.all_to_all(right_noise, ANSWER, split_axis=1, concat_axis=0, tiled=True)
    columns = (right_part.astype(jnp.float32).T * RIGHT_SCALE).astype(jnp.float16)
    rows = pieces(scores * score_scale).reshape(3 * near, block)
    filler = jnp.zeros((-(tile_cols + 3 * near) % 16, block), jnp.float16)
    gathered = lax.all_gather(jnp.concatenate([columns, rows, filler]), "depth", axis=0)

    all_scores = gathered[:, tile_cols : tile_cols + 3 * near].reshape(depth, 3, near, block)
    all_scores = joined(jnp.moveaxis(all_scores, 1, 0)) / score_scale
    average = jnp.sum(all_scores) / population
    variance = jnp.sum(all_scores * all_scores) / population - average * average
    fitness = (all_scores - average) / jnp.sqrt(variance + 1e-05)
    fitness = lax.dynamic_index_in_dim(fitness, near_place, 1, keepdims=False)
    fitness = (fitness / RIGHT_SCALE).reshape(depth, answers, share)

    weighted = left_rows.transpose(2, 1, 3, 0, 4).astype(jnp.float32) * fitness[..., None, None]
    weighted = weighted.astype(jnp.bfloat16).reshape(depth, block, near * tile_rows)
    partial_update = lax.dot_general(
        weighted,
        gathered[:, :tile_cols].astype(jnp.bfloat16),
        (((0, 1), (0, 2)), ((), ())),
        preferred_element_type=jnp.float32,
    )
    partial_update = partial_update.reshape(near, tile_rows, tile_cols)
    kept = lax.dynamic_index_in_dim(partial_update, near_place, 0, keepdims=False)
    sent = lax.dynamic_index_in_dim(partial_update, 1 - near_place, 0, keepdims=False)
    received = lax.ppermute(sent.astype(jnp.bfloat16), "near", [(0, 1), (1, 0)])
    update = kept + received.astype(jnp.float32)
    new_master = master + update / jnp.sqrt(jnp.float32(population))
    rollout = lax.all_to_all(
        new_master.astype(jnp.bfloat16), ANSWER, split_axis=0, concat_axis=1, tiled=True
    )
    return (new_master, rollout)


def solution(mesh):
    finer = Mesh(
        mesh.devices.reshape(-1, 2, 2, mesh.shape["tensor"] // 2, mesh.shape["answer"]),
        (*MEMBER, *TENSOR, ANSWER),
    )
    placed = (
        P(MEMBER, (*TENSOR, ANSWER)),
        P((*MEMBER, ANSWER), None),
        P((*MEMBER, ANSWER), TENSOR),
        P(MEMBER, ANSWER),
    )
    return jax.shard_map(
        body,
        mesh=finer,
        in_specs=placed,
        out_specs=(P(MEMBER, (*TENSOR, ANSWER)), P((*MEMBER, ANSWER), TENSOR)),
        check_vma=False,
    )
```

time: 155 us -> 154 us (level)
  blocking collectives: 28.8 us -> 66.7 us
  waiting for transfers between devices: 64.1 us -> 27.1 us
  between operations: 16.9 us -> 3.43 us
  local copies, waits for them, and re-layouts: 8.18 us -> 17.1 us
    all_gather x0 -> x1, blocking collectives: none -> 55 us  [body(): lax.all_gather(jnp.concatenate([columns, rows, filler]), 'depth', axis=0)]
    all_to_all x2, waiting for transfers between devices: 22.9 us -> 2.78 us  [spread(): return lax.all_to_all(copies, axes, 0, 0, tiled=True)]
    all_gather x1 -> x0, waiting for transfers between devices: 19.6 us -> none  [body(): right_cols = lax.all_gather(right_part, 'depth', axis=0, tiled=True)]
    psum x1 -> x0, blocking collectives: 8.9 us -> none  [body(): scores = lax.psum(jnp.sum(returns, axis=1), 'answer')]
    all_to_all x2 -> x1, blocking collectives: 19.9 us -> 11.7 us  [body(): lax.all_to_all(new_master.astype(jnp.bfloat16), ANSWER, split_axis=0, con...]
    reshape x0 -> x2, local copies, waits for them, and re-layouts: none -> 3.56 us  [the longest x1 2 us: body(): weighted.astype(jnp.bfloat16).reshape(depth, block, near * tile_rows)]
    all_to_all x1 -> x2, starting transfers between devices: 15.2 us -> 18.6 us  [the longest x1 15.2 us: body(): half = lax.all_to_all(half.transpose(1, 0, 2), 'depth', 0, 0, tiled=True)]
    all_to_all x1 -> x2, waiting for transfers between devices: 15.8 us -> 19.1 us  [the longest x1 16 us: body(): half = lax.all_to_all(half.transpose(1, 0, 2), 'depth', 0, 0, tiled=True)]
  transfers between devices with their start and end apart: 5 -> 5, of which waited for: 5 -> 4; matrix products, arithmetic and copies ran while one was open for 4% -> 3% of each run, Pallas kernels for 0% -> 0%
where the time goes in v2:
time: 154 us; the launch traced here: 152 us
  blocking collectives  66.7 us (43%)
  starting transfers between devices  31.5 us (20%)
  waiting for transfers between devices  27.1 us (18%)
  local copies, waits for them, and re-layouts  17.1 us (11%)
  matrix products  3.62 us (2%)
  between operations  3.43 us (2%)
  other arithmetic  3.16 us (2%)
    all_gather x1, blocking collectives, body(): lax.all_gather(jnp.concatenate([columns, rows, filler]), 'depth', axis=0)  55 us
    all_to_all x1, waiting for transfers between devices, body(): half = lax.all_to_all(half.transpose(1, 0, 2), 'depth', 0, 0, tiled=True)  16 us
    all_to_all x1, starting transfers between devices, body(): half = lax.all_to_all(half.transpose(1, 0, 2), 'depth', 0, 0, tiled=True)  15.2 us
    all_to_all x1, blocking collectives, body(): lax.all_to_all(new_master.astype(jnp.bfloat16), ANSWER, split_axis=0, con...  11.7 us
    all_to_all x2, starting transfers between devices, spread(): return lax.all_to_all(copies, axes, 0, 0, tiled=True)  9.53 us
    ppermute x1, waiting for transfers between devices, body(): received = lax.ppermute(sent.astype(jnp.bfloat16), 'near', [(0, 1), (1, 0)])  5.15 us
    dot_general x1, matrix products, body(): lax.dot_general(weighted, gathered[:, :tile_cols].astype(jnp.bfloat16), (...  3.62 us
    all_to_all x1, starting transfers between devices, body(): lax.all_to_all(right_noise, ANSWER, split_axis=1, concat_axis=0, tiled=True)  3.39 us
  transfers between devices with their start and end apart: 5, of which 4 were waited for; matrix products, arithmetic and copies ran while one was open for 3% of the time, Pallas kernels for 0%

profile of v2, /device:TPU:6, one launch (start us, length us, event | category | flops | bytes accessed | tf_op | source)
XLA Modules:
  0.0 152.5 jit_solution(646338607970012950)
XLA Ops:
  0.6 0.9 reduce_sum.36
  2.2 5.9 %all-to-all-start.3 = ((f32[8,1,128]{2,1,0:T(1,128)}), f32[8,1,128]{2,1,0:T(1,128)S(1)}, u32[]{:S(2)}, u32[]{:S(2)}) async-start(f32[8,1,128]{2,1,0:T(1,128)} %broadcast_in_dim.7), calls=%async_computation.3 | async-start | bytes 8192 | tf_op jit(solution)/shard_map/all_to_all | solution.py:18
  8.1 1.1 all_to_all.36
  9.2 0.7 copy.47
  10.0 2.8 %all-to-all-done.3 = f32[8,1,128]{2,1,0:T(1,128)S(1)} async-done(((f32[8,1,128]{2,1,0:T(1,128)}), f32[8,1,128]{2,1,0:T(1,128)S(1)}, u32[]{:S(2)}, u32[]{:S(2)}) %all-to-all-start.3) | async-done | bytes 4128 | tf_op jit(solution)/shard_map/all_to_all | solution.py:18
  12.7 3.4 %all-to-all-start.2 = ((bf16[32,4,864]{2,0,1:T(8,128)(2,1)}), bf16[32,4,864]{2,0,1:T(8,128)(2,1)S(1)}, u32[]{:S(2)}, u32[]{:S(2)}) async-start(bf16[32,4,864]{2,0,1:T(8,128)(2,1)} %copy.47), calls=%async_computation.2 | async-start | bytes 458752 | tf_op jit(solution)/shard_map/all_to_all | solution.py:51
  16.1 1.6 %reshape.94 = bf16[32,16,2,160]{3,2,1,0:T(2,128)(2,1)S(1)} reshape(bf16[32,5120]{1,0:T(8,128)(2,1)} %param.5) | data formatting | bytes 655360 | tf_op jit(solution)/shard_map/reshape | solution.py:43
  18.3 1.0 copy.62
  19.4 3.2 %all-to-all-done.2 = bf16[32,4,864]{2,0,1:T(8,128)(2,1)S(1)} async-done(((bf16[32,4,864]{2,0,1:T(8,128)(2,1)}), bf16[32,4,864]{2,0,1:T(8,128)(2,1)S(1)}, u32[]{:S(2)}, u32[]{:S(2)}) %all-to-all-start.2) | async-done | bytes 221216 | tf_op jit(solution)/shard_map/all_to_all | solution.py:51
  22.6 15.2 %all-to-all-start = ((bf16[16,32,160]{2,1,0:T(8,128)(2,1)}), bf16[16,32,160]{2,1,0:T(8,128)(2,1)S(1)}, u32[]{:S(2)}, u32[]{:S(2)}) async-start(bf16[16,32,160]{2,1,0:T(8,128)(2,1)} %bitcast.55), calls=%async_computation | async-start | bytes 524288 | tf_op jit(solution)/shard_map/all_to_all | solution.py:45
  38.4 16.0 %all-to-all-done = bf16[16,32,160]{2,1,0:T(8,128)(2,1)S(1)} async-done(((bf16[16,32,160]{2,1,0:T(8,128)(2,1)}), bf16[16,32,160]{2,1,0:T(8,128)(2,1)S(1)}, u32[]{:S(2)}, u32[]{:S(2)}) %all-to-all-start) | async-done | bytes 163872 | tf_op jit(solution)/shard_map/all_to_all | solution.py:45
  54.4 1.6 %broadcast_in_dim.6 = bf16[8,16,32,160]{3,2,1,0:T(8,128)(2,1)} broadcast(bf16[16,32,160]{2,1,0:T(8,128)(2,1)S(1)} %all-to-all-done), dimensions={1,2,3} | broadcast | bytes 1474560 | tf_op jit(solution)/shard_map/broadcast_in_dim | solution.py:17
  56.0 3.6 %all-to-all-start.1 = ((bf16[8,16,32,160]{3,2,1,0:T(8,128)(2,1)}), bf16[8,16,32,160]{3,2,1,0:T(8,128)(2,1)S(1)}, u32[]{:S(2)}, u32[]{:S(2)}) async-start(bf16[8,16,32,160]{3,2,1,0:T(8,128)(2,1)} %broadcast_in_dim.6), calls=%async_computation.1 | async-start | bytes 4194304 | tf_op jit(solution)/shard_map/all_to_all | solution.py:18
  59.6 55.0 %all-gather.2 = f16[14080,128]{1,0:T(8,128)(2,1)S(1)} all-gather(f16[880,128]{1,0:T(8,128)(2,1)S(1)} %copy.49), channel_id=2, replica_groups=mesh['depth'=16,'near'=2,'far'=2,'core'=2,'answer'=4] {'depth'}, dimensions={0}, use_global_device_ids=true | all-gather | bytes 3829760 | tf_op jit(solution)/shard_map/all_gather | solution.py:55
  114.6 1.8 %copy-done = f16[14080,128]{1,0:T(8,128)(2,1)} copy-done((f16[14080,128]{1,0:T(8,128)(2,1)}, f16[14080,128]{1,0:T(8,128)(2,1)S(1)}, u32[]{:S(2)}) %copy-start) | copy-done | bytes 3604504
  120.2 2.2 %copy.52 = bf16[16,4,32,2,160]{4,3,2,1,0:T(2,128)(2,1)S(1)} copy(bf16[16,4,32,2,160]{4,2,0,1,3:T(8,128)(2,1)S(1)} %fusion.1) | data formatting | bytes 2621440 | tf_op jit(solution)/shard_map/convert_element_type | solution.py:66
  122.4 2.0 %reshape.97 = bf16[16,128,320]{2,1,0:T(8,128)(2,1)} reshape(bf16[16,4,32,2,160]{4,3,2,1,0:T(2,128)(2,1)S(1)} %copy.52) | data formatting | bytes 2621440 | tf_op jit(solution)/shard_map/reshape | solution.py:66
  124.4 2.2 %copy.53 = bf16[320,16,128]{2,1,0:T(8,128)(2,1)S(1)} copy(bf16[320,16,128]{0,2,1:T(8,128)(2,1)} %bitcast.57) | data formatting | bytes 2621440 | tf_op jit(solution)/shard_map/dot_general | solution.py:67
  126.6 3.6 %fusion.5 = f32[2,160,864]{2,1,0:T(8,128)S(1)} fusion(f16[16,880,128]{2,1,0:T(8,128)(2,1)} %bitcast.59, bf16[2,160,16,128]{3,2,1,0:T(8,128)(2,1)S(1)} %bitcast.60), kind=kOutput, calls=%fused_computation.6 | convolution fusion | flops 1134231552 | bytes 5955584 | tf_op jit(solution)/shard_map/dot_general | solution.py:67
  130.3 3.4 %collective-permute-start = (bf16[160,864]{1,0:T(8,128)(2,1)S(1)}, bf16[160,864]{1,0:T(8,128)(2,1)S(1)}, u32[]{:S(2)}, u32[]{:S(2)}) collective-permute-start(bf16[160,864]{1,0:T(8,128)(2,1)S(1)} %fusion.11), channel_id=1, source_target_pairs={{0,16},{16,0},{1,17},{17,1},{2,18},{18,2},{3,19},{19,3},{4,20},{20... | collective-permute-start | bytes 829448 | tf_op jit(solution)/shard_map/ppermute | solution.py:76
  133.6 5.2 %collective-permute-done = bf16[160,864]{1,0:T(8,128)(2,1)S(1)} collective-permute-done((bf16[160,864]{1,0:T(8,128)(2,1)S(1)}, bf16[160,864]{1,0:T(8,128)(2,1)S(1)}, u32[]{:S(2)}, u32[]{:S(2)}) %collective-permute-start) | collective-permute-done | bytes 276512 | tf_op jit(solution)/shard_map/ppermute | solution.py:76
  138.8 0.9 fusion.18
  139.7 11.7 %all_to_all.48 = bf16[4,40,864]{2,1,0:T(8,128)(2,1)S(1)} all-to-all(bf16[4,40,864]{2,1,0:T(8,128)(2,1)S(1)} %bitcast.61), channel_id=1, replica_groups=mesh['depth'=16,'near'=2,'far'=2,'core'=2,'answer'=4] {'answer'}, dimensions={0} | all-to-all | bytes 552960 | tf_op jit(solution)/shard_map/all_to_all | solution.py:79
  151.5 0.9 all_to_all.42
  (25 shorter events, 3.3 us)
Async XLA Ops:
  2.2 10.5 %all-to-all-start.3 = ((f32[8,1,128]{2,1,0:T(1,128)}), f32[8,1,128]{2,1,0:T(1,128)S(1)}, u32[]{:S(2)}, u32[]{:S(2)}) async-start(f32[8,1,128]{2,1,0:T(1,128)} %broadcast_in_dim.7), calls=%async_computation.3 | async-start | bytes 8192 | tf_op jit(solution)/shard_map/all_to_all | solution.py:18
  12.7 9.9 %all-to-all-start.2 = ((bf16[32,4,864]{2,0,1:T(8,128)(2,1)}), bf16[32,4,864]{2,0,1:T(8,128)(2,1)S(1)}, u32[]{:S(2)}, u32[]{:S(2)}) async-start(bf16[32,4,864]{2,0,1:T(8,128)(2,1)} %copy.47), calls=%async_computation.2 | async-start | bytes 458752 | tf_op jit(solution)/shard_map/all_to_all | solution.py:51
  22.6 31.8 %all-to-all-start = ((bf16[16,32,160]{2,1,0:T(8,128)(2,1)}), bf16[16,32,160]{2,1,0:T(8,128)(2,1)S(1)}, u32[]{:S(2)}, u32[]{:S(2)}) async-start(bf16[16,32,160]{2,1,0:T(8,128)(2,1)} %bitcast.55), calls=%async_computation | async-start | bytes 524288 | tf_op jit(solution)/shard_map/all_to_all | solution.py:45
  56.0 63.7 %all-to-all-start.1 = ((bf16[8,16,32,160]{3,2,1,0:T(8,128)(2,1)}), bf16[8,16,32,160]{3,2,1,0:T(8,128)(2,1)S(1)}, u32[]{:S(2)}, u32[]{:S(2)}) async-start(bf16[8,16,32,160]{3,2,1,0:T(8,128)(2,1)} %broadcast_in_dim.6), calls=%async_computation.1 | async-start | bytes 4194304 | tf_op jit(solution)/shard_map/all_to_all | solution.py:18
  114.6 1.8 %copy-start = (f16[14080,128]{1,0:T(8,128)(2,1)}, f16[14080,128]{1,0:T(8,128)(2,1)S(1)}, u32[]{:S(2)}) copy-start(f16[14080,128]{1,0:T(8,128)(2,1)S(1)} %all-gather.2) | copy-start | bytes 10813444
  126.6 12.2 %copy-start.1 = (f32[160,864]{1,0:T(8,128)S(1)}, f32[160,864]{1,0:T(8,128)}, u32[]{:S(2)}) copy-start(f32[160,864]{1,0:T(8,128)} %param.4) | copy-start | bytes 1658884
  130.3 8.5 %collective-permute-start = (bf16[160,864]{1,0:T(8,128)(2,1)S(1)}, bf16[160,864]{1,0:T(8,128)(2,1)S(1)}, u32[]{:S(2)}, u32[]{:S(2)}) collective-permute-start(bf16[160,864]{1,0:T(8,128)(2,1)S(1)} %fusion.11), channel_id=1, source_target_pairs={{0,16},{16,0},{1,17},{17,1},{2,18},{18,2},{3,19},{19,3},{4,20},{20... | collective-permute-start | bytes 829448 | tf_op jit(solution)/shard_map/ppermute | solution.py:76

commit v3 on v2

--- a/solution.py
+++ b/solution.py
@@ -40,15 +40,36 @@
     near_place = lax.axis_index("near")
     score_scale = 2.0 ** math.floor(math.log2(32768.0 / (12.0 * answers * returns.shape[1])))
 
-    half = left_noise.reshape(share, depth, cores, -1)
-    half = lax.dynamic_index_in_dim(half, lax.axis_index("core"), 2, keepdims=False)
-    half = lax.all_to_all(half.transpose(1, 0, 2), "depth", 0, 0, tiled=True)
-    left_rows = spread(half, ("core", ANSWER)).reshape(cores, answers, depth, share, -1)
+    half = lax.dynamic_slice_in_dim(
+        left_noise, lax.axis_index("core") * (share // cores), share // cores, 0
+    )
+    half = half.reshape(share // cores, depth, -1).transpose(1, 0, 2)
+    half, right_noise, returns = lax.optimization_barrier((half, right_noise, returns))
+    half = lax.all_to_all(half, "depth", 0, 0, tiled=True)
+    left_rows = spread(half, ("core", ANSWER)).reshape(cores, answers, depth, share // cores, -1)
 
-    partial_scores = spread(jnp.sum(returns, axis=1), ("near", ANSWER))
-    scores = jnp.sum(partial_scores.reshape(near, answers, block), axis=1)
+    answer_place = lax.axis_index(ANSWER)
+    outgoing = right_noise.reshape(share, answers, tile_cols).transpose(1, 0, 2)
+    incoming = []
+    for step in range(answers):
+        part = lax.dynamic_index_in_dim(
+            outgoing, (answer_place + step) % answers, 0, keepdims=False
+        )
+        hops = [(i, (i + step) % answers) for i in range(answers)]
+        incoming.append(lax.ppermute(part, ANSWER, hops) if step else part)
+    incoming = jnp.stack(incoming)
+    right_part = jnp.concatenate(
+        [
+            lax.dynamic_index_in_dim(
+                incoming, (answer_place - i) % answers, 0, keepdims=False
+            )
+            for i in range(answers)
+        ]
+    )
+    scores = jnp.zeros((near, block), jnp.float32)
+    scores = lax.dynamic_update_index_in_dim(scores, jnp.sum(returns, axis=1), near_place, 0)
+    scores = lax.psum(scores, ("near", ANSWER))
 
-    right_part = lax.all_to_all(right_noise, ANSWER, split_axis=1, concat_axis=0, tiled=True)
     columns = (right_part.astype(jnp.float32).T * RIGHT_SCALE).astype(jnp.float16)
     rows = pieces(scores * score_scale).reshape(3 * near, block)
     filler = jnp.zeros((-(tile_cols + 3 * near) % 16, block), jnp.float16)
@@ -60,25 +81,31 @@
     variance = jnp.sum(all_scores * all_scores) / population - average * average
     fitness = (all_scores - average) / jnp.sqrt(variance + 1e-05)
     fitness = lax.dynamic_index_in_dim(fitness, near_place, 1, keepdims=False)
-    fitness = (fitness / RIGHT_SCALE).reshape(depth, answers, share)
+    fitness = fitness / (RIGHT_SCALE * math.sqrt(population))
 
-    weighted = left_rows.transpose(2, 1, 3, 0, 4).astype(jnp.float32) * fitness[..., None, None]
-    weighted = weighted.astype(jnp.bfloat16).reshape(depth, block, near * tile_rows)
+    weighted = gathered[:, :tile_cols].astype(jnp.float32) * fitness[:, None]
+    left_rows = left_rows.transpose(2, 1, 0, 3, 4).reshape(depth, block, near * tile_rows)
     partial_update = lax.dot_general(
-        weighted,
-        gathered[:, :tile_cols].astype(jnp.bfloat16),
+        left_rows,
+        weighted.astype(jnp.bfloat16),
         (((0, 1), (0, 2)), ((), ())),
         preferred_element_type=jnp.float32,
     )
-    partial_update = partial_update.reshape(near, tile_rows, tile_cols)
-    kept = lax.dynamic_index_in_dim(partial_update, near_place, 0, keepdims=False)
-    sent = lax.dynamic_index_in_dim(partial_update, 1 - near_place, 0, keepdims=False)
-    received = lax.ppermute(sent.astype(jnp.bfloat16), "near", [(0, 1), (1, 0)])
-    update = kept + received.astype(jnp.float32)
-    new_master = master + update / jnp.sqrt(jnp.float32(population))
-    rollout = lax.all_to_all(
-        new_master.astype(jnp.bfloat16), ANSWER, split_axis=0, concat_axis=1, tiled=True
-    )
+    kept = lax.dynamic_slice_in_dim(partial_update, near_place * tile_rows, tile_rows, 0)
+    sent = lax.dynamic_slice_in_dim(partial_update, (1 - near_place) * tile_rows, tile_rows, 0)
+    sent = sent.astype(jnp.bfloat16)
+    received = lax.ppermute(sent, "near", [(0, 1), (1, 0)])
+    kept = master + kept
+
+    parts = kept.astype(jnp.bfloat16)
+    parts = jnp.where(near_place == 0, jnp.stack([parts, sent]), jnp.stack([sent, parts]))
+    parts = parts.reshape(near * answers, -1, tile_cols)
+    parts = lax.all_to_all(parts, ("near", ANSWER), 0, 0, tiled=True)
+    parts, received, kept = lax.optimization_barrier((parts, received, kept))
+    new_master = kept + received.astype(jnp.float32)
+    parts = parts.reshape(near, answers, -1, tile_cols).astype(jnp.float32)
+    rollout = (parts[0] + parts[1]).astype(jnp.bfloat16)
+    rollout = rollout.transpose(1, 0, 2).reshape(-1, answers * tile_cols)
     return (new_master, rollout)
 
 

time: 154 us -> 140 us (0.909)
  waiting for transfers between devices: 27.1 us -> 6.62 us
  local copies, waits for them, and re-layouts: 17.1 us -> 7.61 us
  blocking collectives: 66.7 us -> 75.6 us
  starting transfers between devices: 31.5 us -> 38 us
    all_to_all x2, waiting for transfers between devices: 19.1 us -> 0.01 us  [the longest x1 0.01 us: body(): half = lax.all_to_all(half, 'depth', 0, 0, tiled=True)]
    psum x0 -> x1, blocking collectives: none -> 18.5 us  [body(): scores = lax.psum(scores, ('near', ANSWER))]
    all_to_all x1 -> x0, blocking collectives: 11.7 us -> none  [body(): lax.all_to_all(new_master.astype(jnp.bfloat16), ANSWER, split_axis=0, con...]
    ppermute x1 -> x4, starting transfers between devices: 3.37 us -> 12.3 us  [the longest x3 10.3 us: body(): incoming.append(lax.ppermute(part, ANSWER, hops) if step else part)]
    all_to_all x2 -> x1, starting transfers between devices: 9.53 us -> 3.58 us  [spread(): return lax.all_to_all(copies, axes, 0, 0, tiled=True)]
    all_to_all x2, starting transfers between devices: 18.6 us -> 22.1 us  [the longest x1 15.2 us: body(): half = lax.all_to_all(half, 'depth', 0, 0, tiled=True)]
    all_to_all x4 -> x0, local copies, waits for them, and re-layouts: 2.89 us -> none  [the longest x2 1.84 us: body(): lax.all_to_all(right_noise, ANSWER, split_axis=1, concat_axis=0, tiled=True)]
    all_to_all x2 -> x1, waiting for transfers between devices: 2.78 us -> 0.01 us  [spread(): return lax.all_to_all(copies, axes, 0, 0, tiled=True)]
  transfers between devices with their start and end apart: 5 -> 7, of which waited for: 4 -> 1; matrix products, arithmetic and copies ran while one was open for 3% -> 2% of each run, Pallas kernels for 0% -> 0%
where the time goes in v3:
time: 140 us; the launch traced here: 138 us
  blocking collectives  75.6 us (54%)
  starting transfers between devices  38 us (27%)
  local copies, waits for them, and re-layouts  7.61 us (5%)
  waiting for transfers between devices  6.62 us (5%)
  matrix products  3.96 us (3%)
  between operations  3.73 us (3%)
  other arithmetic  2.98 us (2%)
    all_gather x1, blocking collectives, body(): lax.all_gather(jnp.concatenate([columns, rows, filler]), 'depth', axis=0)  57.2 us
    psum x1, blocking collectives, body(): scores = lax.psum(scores, ('near', ANSWER))  18.5 us
    all_to_all x1, starting transfers between devices, body(): half = lax.all_to_all(half, 'depth', 0, 0, tiled=True)  15.2 us
    ppermute x3, starting transfers between devices, body(): incoming.append(lax.ppermute(part, ANSWER, hops) if step else part)  10.3 us
    all_to_all x1, starting transfers between devices, body(): parts = lax.all_to_all(parts, ('near', ANSWER), 0, 0, tiled=True)  6.92 us
    ppermute x1, waiting for transfers between devices, body(): received = lax.ppermute(sent, 'near', [(0, 1), (1, 0)])  6.6 us
    dot_general x1, matrix products, body(): lax.dot_general(left_rows, weighted.astype(jnp.bfloat16), (((0, 1), (0, 2...  3.96 us
    all_to_all x1, starting transfers between devices, spread(): return lax.all_to_all(copies, axes, 0, 0, tiled=True)  3.58 us
  transfers between devices with their start and end apart: 7, of which 1 were waited for; matrix products, arithmetic and copies ran while one was open for 2% of the time, Pallas kernels for 0%

profile of v3, /device:TPU:6, one launch (start us, length us, event | category | flops | bytes accessed | tf_op | source)
XLA Modules:
  0.0 138.5 jit_solution(12764008534993342768)
XLA Ops:
  0.7 0.9 copy-done
  1.6 0.2 reshape.56
  1.8 0.7 copy.30
  2.5 15.2 %all-to-all-start = ((bf16[16,16,320]{2,1,0:T(8,128)(2,1)}), bf16[16,16,320]{2,1,0:T(8,128)(2,1)S(1)}, u32[]{:S(2)}, u32[]{:S(2)}) async-start(bf16[16,16,320]{2,1,0:T(8,128)(2,1)} %copy.30), calls=%async_computation | async-start | bytes 393216 | tf_op jit(solution)/shard_map/all_to_all | solution.py:48
  17.8 0.2 reshape.59
  18.0 0.5 constant_dynamic-slice_fusion.3
  18.5 4.9 %collective-permute-start.2 = (bf16[32,864]{1,0:T(8,128)(2,1)S(1)}, bf16[32,864]{1,0:T(8,128)(2,1)S(1)}, u32[]{:S(2)}, u32[]{:S(2)}) collective-permute-start(bf16[32,864]{1,0:T(8,128)(2,1)S(1)} %bitcast.63), channel_id=1, source_target_pairs={{0,3},{1,0},{2,1},{3,2},{4,7},{5,4},{6,5},{7,6},{8,11},{9,8},{10,9... | collective-permute-start | bytes 165896 | tf_op jit(solution)/shard_map/ppermute | solution.py:59
  23.5 2.5 %collective-permute-start.1 = (bf16[32,864]{1,0:T(8,128)(2,1)S(1)}, bf16[32,864]{1,0:T(8,128)(2,1)S(1)}, u32[]{:S(2)}, u32[]{:S(2)}) collective-permute-start(bf16[32,864]{1,0:T(8,128)(2,1)S(1)} %bitcast.64), channel_id=1, source_target_pairs={{0,2},{1,3},{2,0},{3,1},{4,6},{5,7},{6,4},{7,5},{8,10},{9,11},{10,... | collective-permute-start | bytes 165896 | tf_op jit(solution)/shard_map/ppermute | solution.py:59
  26.0 2.9 %collective-permute-start = (bf16[32,864]{1,0:T(8,128)(2,1)S(1)}, bf16[32,864]{1,0:T(8,128)(2,1)S(1)}, u32[]{:S(2)}, u32[]{:S(2)}) collective-permute-start(bf16[32,864]{1,0:T(8,128)(2,1)S(1)} %bitcast.65), channel_id=1, source_target_pairs={{0,1},{1,2},{2,3},{3,0},{4,5},{5,6},{6,7},{7,4},{8,9},{9,10},{10,1... | collective-permute-start | bytes 165896 | tf_op jit(solution)/shard_map/ppermute | solution.py:59
  29.1 18.5 %psum.7 = f32[2,128]{1,0:T(2,128)S(1)} all-reduce(f32[2,128]{1,0:T(2,128)S(1)} %dynamic_update_slice.4), channel_id=1, replica_groups=mesh['depth'=16,'near'=2,'far'=2,'core'=2,'answer'=4] {'near','answer'}, use_global_device_ids=true, to_apply=%region_1.2 | all-reduce | flops 256 | bytes 2048 | tf_op jit(solution)/shard_map/psum | solution.py:71
  48.2 0.3 copy.33
  48.5 1.3 broadcast_in_dim.17
  49.8 3.6 %all-to-all-start.1 = ((bf16[8,16,16,320]{3,2,1,0:T(8,128)(2,1)}), bf16[8,16,16,320]{3,2,1,0:T(8,128)(2,1)S(1)}, u32[]{:S(2)}, u32[]{:S(2)}) async-start(bf16[8,16,16,320]{3,2,1,0:T(8,128)(2,1)} %broadcast_in_dim.17), calls=%async_computation.1 | async-start | bytes 3145728 | tf_op jit(solution)/shard_map/all_to_all | solution.py:18
  53.4 57.2 %all-gather.2 = f16[14080,128]{1,0:T(8,128)(2,1)S(1)} all-gather(f16[880,128]{1,0:T(8,128)(2,1)S(1)} %copy.33), channel_id=2, replica_groups=mesh['depth'=16,'near'=2,'far'=2,'core'=2,'answer'=4] {'depth'}, dimensions={0}, use_global_device_ids=true | all-gather | bytes 3829760 | tf_op jit(solution)/shard_map/all_gather | solution.py:76
  110.5 1.8 %copy-done.1 = f16[14080,128]{1,0:T(8,128)(2,1)} copy-done((f16[14080,128]{1,0:T(8,128)(2,1)}, f16[14080,128]{1,0:T(8,128)(2,1)S(1)}, u32[]{:S(2)}) %copy-start.1) | copy-done | bytes 3604504
  112.3 0.6 fusion.16
  115.6 0.2 copy.31
  115.9 4.0 %fusion.3 = f32[320,864]{1,0:T(8,128)S(1)} fusion(bf16[16,128,320]{2,1,0:T(8,128)(2,1)S(1)} %bitcast.56, f16[16,880,128]{2,1,0:T(8,128)(2,1)} %bitcast.55, f32[16,128]{1,0:T(8,128)S(1)} %fusion.9), kind=kOutput, calls=%fused_computation.4 | convolution fusion | flops 1137770496 | bytes 5963776 | tf_op jit(solution)/shard_map/dot_general | solution.py:88
  120.0 0.9 maximum_select_fusion
  120.9 6.9 %all-to-all-start.2 = ((bf16[8,40,864]{2,1,0:T(8,128)(2,1)}), bf16[8,40,864]{2,1,0:T(8,128)(2,1)S(1)}, u32[]{:S(2)}, u32[]{:S(2)}) async-start(bf16[8,40,864]{2,1,0:T(8,128)(2,1)} %bitcast.24), calls=%async_computation.2 | async-start | bytes 1146880 | tf_op jit(solution)/shard_map/all_to_all | solution.py:103
  127.9 1.9 %collective-permute-start.3 = (bf16[160,864]{1,0:T(8,128)(2,1)S(1)}, bf16[160,864]{1,0:T(8,128)(2,1)S(1)}, u32[]{:S(2)}, u32[]{:S(2)}) collective-permute-start(bf16[160,864]{1,0:T(8,128)(2,1)S(1)} %dynamic-slice_convert_fusion), channel_id=1, source_target_pairs={{0,16},{16,0},{1,17},{17,1},{2,18},{18,2},{3,19},{19,3},{4,20},{20... | collective-permute-start | bytes 829448 | tf_op jit(solution)/shard_map/ppermute | solution.py:97
  129.8 6.6 %collective-permute-done.3 = bf16[160,864]{1,0:T(8,128)(2,1)S(1)} collective-permute-done((bf16[160,864]{1,0:T(8,128)(2,1)S(1)}, bf16[160,864]{1,0:T(8,128)(2,1)S(1)}, u32[]{:S(2)}, u32[]{:S(2)}) %collective-permute-start.3) | collective-permute-done | bytes 276512 | tf_op jit(solution)/shard_map/ppermute | solution.py:97
  136.7 0.9 reshape.61
  137.6 0.9 convert_add_fusion
  (41 shorter events, 1.2 us)
Async XLA Ops:
  0.6 1.0 copy-start
  0.6 17.1 %copy-start.3 = (bf16[32,3456]{1,0:T(8,128)(2,1)S(1)}, bf16[32,3456]{1,0:T(8,128)(2,1)}, u32[]{:S(2)}) copy-start(bf16[32,3456]{1,0:T(8,128)(2,1)} %param.6) | copy-start | bytes 663556
  1.6 27.3 %copy-start.4 = (f32[128,128]{1,0:T(8,128)S(1)}, f32[128,128]{1,0:T(8,128)}, u32[]{:S(2)}) copy-start(f32[128,128]{1,0:T(8,128)} %param.7) | copy-start | bytes 196612
  2.5 46.0 %all-to-all-start = ((bf16[16,16,320]{2,1,0:T(8,128)(2,1)}), bf16[16,16,320]{2,1,0:T(8,128)(2,1)S(1)}, u32[]{:S(2)}, u32[]{:S(2)}) async-start(bf16[16,16,320]{2,1,0:T(8,128)(2,1)} %copy.30), calls=%async_computation | async-start | bytes 393216 | tf_op jit(solution)/shard_map/all_to_all | solution.py:48
  18.5 29.4 %collective-permute-start.2 = (bf16[32,864]{1,0:T(8,128)(2,1)S(1)}, bf16[32,864]{1,0:T(8,128)(2,1)S(1)}, u32[]{:S(2)}, u32[]{:S(2)}) collective-permute-start(bf16[32,864]{1,0:T(8,128)(2,1)S(1)} %bitcast.63), channel_id=1, source_target_pairs={{0,3},{1,0},{2,1},{3,2},{4,7},{5,4},{6,5},{7,6},{8,11},{9,8},{10,9... | collective-permute-start | bytes 165896 | tf_op jit(solution)/shard_map/ppermute | solution.py:59
  23.5 24.5 %collective-permute-start.1 = (bf16[32,864]{1,0:T(8,128)(2,1)S(1)}, bf16[32,864]{1,0:T(8,128)(2,1)S(1)}, u32[]{:S(2)}, u32[]{:S(2)}) collective-permute-start(bf16[32,864]{1,0:T(8,128)(2,1)S(1)} %bitcast.64), channel_id=1, source_target_pairs={{0,2},{1,3},{2,0},{3,1},{4,6},{5,7},{6,4},{7,5},{8,10},{9,11},{10,... | collective-permute-start | bytes 165896 | tf_op jit(solution)/shard_map/ppermute | solution.py:59
  26.0 21.9 %collective-permute-start = (bf16[32,864]{1,0:T(8,128)(2,1)S(1)}, bf16[32,864]{1,0:T(8,128)(2,1)S(1)}, u32[]{:S(2)}, u32[]{:S(2)}) collective-permute-start(bf16[32,864]{1,0:T(8,128)(2,1)S(1)} %bitcast.65), channel_id=1, source_target_pairs={{0,1},{1,2},{2,3},{3,0},{4,5},{5,6},{6,7},{7,4},{8,9},{9,10},{10,1... | collective-permute-start | bytes 165896 | tf_op jit(solution)/shard_map/ppermute | solution.py:59
  49.8 65.8 %all-to-all-start.1 = ((bf16[8,16,16,320]{3,2,1,0:T(8,128)(2,1)}), bf16[8,16,16,320]{3,2,1,0:T(8,128)(2,1)S(1)}, u32[]{:S(2)}, u32[]{:S(2)}) async-start(bf16[8,16,16,320]{3,2,1,0:T(8,128)(2,1)} %broadcast_in_dim.17), calls=%async_computation.1 | async-start | bytes 3145728 | tf_op jit(solution)/shard_map/all_to_all | solution.py:18
  110.5 1.8 %copy-start.1 = (f16[14080,128]{1,0:T(8,128)(2,1)}, f16[14080,128]{1,0:T(8,128)(2,1)S(1)}, u32[]{:S(2)}) copy-start(f16[14080,128]{1,0:T(8,128)(2,1)S(1)} %all-gather.2) | copy-start | bytes 10813444
  115.9 4.0 %copy-start.2 = (f32[160,864]{1,0:T(8,128)S(1)}, f32[160,864]{1,0:T(8,128)}, u32[]{:S(2)}) copy-start(f32[160,864]{1,0:T(8,128)} %param.4) | copy-start | bytes 1658884
  120.9 15.5 %all-to-all-start.2 = ((bf16[8,40,864]{2,1,0:T(8,128)(2,1)}), bf16[8,40,864]{2,1,0:T(8,128)(2,1)S(1)}, u32[]{:S(2)}, u32[]{:S(2)}) async-start(bf16[8,40,864]{2,1,0:T(8,128)(2,1)} %bitcast.24), calls=%async_computation.2 | async-start | bytes 1146880 | tf_op jit(solution)/shard_map/all_to_all | solution.py:103
  127.9 8.5 %collective-permute-start.3 = (bf16[160,864]{1,0:T(8,128)(2,1)S(1)}, bf16[160,864]{1,0:T(8,128)(2,1)S(1)}, u32[]{:S(2)}, u32[]{:S(2)}) collective-permute-start(bf16[160,864]{1,0:T(8,128)(2,1)S(1)} %dynamic-slice_convert_fusion), channel_id=1, source_target_pairs={{0,16},{16,0},{1,17},{17,1},{2,18},{18,2},{3,19},{19,3},{4,20},{20... | collective-permute-start | bytes 829448 | tf_op jit(solution)/shard_map/ppermute | solution.py:97

commit v4 on v3

--- a/solution.py
+++ b/solution.py
@@ -18,12 +18,11 @@
     return lax.all_to_all(copies, axes, 0, 0, tiled=True)
 
 
-def pieces(value):
-    high = lax.reduce_precision(value, 5, 10)
-    rest = (value - high) * PIECE
-    middle = lax.reduce_precision(rest, 5, 10)
-    low = (rest - middle) * PIECE
-    return jnp.stack([high, middle, low]).astype(jnp.float16)
+def pieces(value, exponent_bits, mantissa_bits, scale):
+    high = lax.reduce_precision(value, exponent_bits, mantissa_bits)
+    rest = (value - high) * scale
+    middle = lax.reduce_precision(rest, exponent_bits, mantissa_bits)
+    return jnp.stack([high, middle, (rest - middle) * scale])
 
 
 def joined(parts):
@@ -50,37 +49,52 @@
 
     answer_place = lax.axis_index(ANSWER)
     outgoing = right_noise.reshape(share, answers, tile_cols).transpose(1, 0, 2)
+    own_scores = jnp.sum(returns, axis=1)
+    near_scores = lax.ppermute(own_scores, "near", [(0, 1), (1, 0)])
+    partial_scores = jnp.where(
+        near_place == 0,
+        jnp.stack([own_scores, near_scores]),
+        jnp.stack([near_scores, own_scores]),
+    )
+    partial_scores = pieces(partial_scores, 8, 7, 1.0).astype(jnp.bfloat16)
+    partial_scores = partial_scores.reshape(share, -1)
     incoming = []
     for step in range(answers):
         part = lax.dynamic_index_in_dim(
             outgoing, (answer_place + step) % answers, 0, keepdims=False
         )
+        part = jnp.concatenate([part, partial_scores], axis=1)
         hops = [(i, (i + step) % answers) for i in range(answers)]
         incoming.append(lax.ppermute(part, ANSWER, hops) if step else part)
     incoming = jnp.stack(incoming)
     right_part = jnp.concatenate(
         [
             lax.dynamic_index_in_dim(
-                incoming, (answer_place - i) % answers, 0, keepdims=False
+                incoming[..., :tile_cols], (answer_place - i) % answers, 0, keepdims=False
             )
             for i in range(answers)
         ]
     )
-    scores = jnp.zeros((near, block), jnp.float32)
-    scores = lax.dynamic_update_index_in_dim(scores, jnp.sum(returns, axis=1), near_place, 0)
-    scores = lax.psum(scores, ("near", ANSWER))
+    scores = incoming[..., tile_cols:].astype(jnp.float32)
+    scores = jnp.sum(scores.reshape(answers, 3, near, block), axis=(0, 1))
 
     columns = (right_part.astype(jnp.float32).T * RIGHT_SCALE).astype(jnp.float16)
-    rows = pieces(scores * score_scale).reshape(3 * near, block)
-    filler = jnp.zeros((-(tile_cols + 3 * near) % 16, block), jnp.float16)
+    rows = pieces(scores * score_scale, 5, 10, PIECE).astype(jnp.float16).reshape(3 * near, block)
+    filler = jnp.zeros((-(tile_cols + 3 * near) % 8, block), jnp.float16)
     gathered = lax.all_gather(jnp.concatenate([columns, rows, filler]), "depth", axis=0)
 
-    all_scores = gathered[:, tile_cols : tile_cols + 3 * near].reshape(depth, 3, near, block)
-    all_scores = joined(jnp.moveaxis(all_scores, 1, 0)) / score_scale
-    average = jnp.sum(all_scores) / population
-    variance = jnp.sum(all_scores * all_scores) / population - average * average
-    fitness = (all_scores - average) / jnp.sqrt(variance + 1e-05)
-    fitness = lax.dynamic_index_in_dim(fitness, near_place, 1, keepdims=False)
+    parts = gathered[:, tile_cols : tile_cols + 3 * near].reshape(depth, 3, near, block)
+    all_scores = joined(jnp.moveaxis(parts, 1, 0)) / score_scale
+    total, square_total = lax.optimization_barrier(
+        tuple(
+            jnp.broadcast_to(jnp.sum(value), (1, block))
+            for value in (all_scores, all_scores * all_scores)
+        )
+    )
+    average = total / population
+    variance = square_total / population - average * average
+    fitness = lax.dynamic_index_in_dim(all_scores, near_place, 1, keepdims=False)
+    fitness = (fitness - average) / jnp.sqrt(variance + 1e-05)
     fitness = fitness / (RIGHT_SCALE * math.sqrt(population))
 
     weighted = gathered[:, :tile_cols].astype(jnp.float32) * fitness[:, None]
@@ -91,14 +105,15 @@
         (((0, 1), (0, 2)), ((), ())),
         preferred_element_type=jnp.float32,
     )
+
+    own_rows = lax.broadcasted_iota(jnp.int32, (near, 1, 1), 0) == near_place
+    parts = partial_update.reshape(near, tile_rows, tile_cols)
+    parts = parts + jnp.where(own_rows, master[None], 0.0)
+    sent = lax.dynamic_slice_in_dim(partial_update, (1 - near_place) * tile_rows, tile_rows, 0)
+    sent, partial_update = lax.optimization_barrier((sent.astype(jnp.bfloat16), partial_update))
+    received = lax.ppermute(sent, "near", [(0, 1), (1, 0)])
     kept = lax.dynamic_slice_in_dim(partial_update, near_place * tile_rows, tile_rows, 0)
-    sent = lax.dynamic_slice_in_dim(partial_update, (1 - near_place) * tile_rows, tile_rows, 0)
-    sent = sent.astype(jnp.bfloat16)
-    received = lax.ppermute(sent, "near", [(0, 1), (1, 0)])
-    kept = master + kept
-
-    parts = kept.astype(jnp.bfloat16)
-    parts = jnp.where(near_place == 0, jnp.stack([parts, sent]), jnp.stack([sent, parts]))
+    parts, kept = lax.optimization_barrier((parts.astype(jnp.bfloat16), master + kept))
     parts = parts.reshape(near * answers, -1, tile_cols)
     parts = lax.all_to_all(parts, ("near", ANSWER), 0, 0, tiled=True)
     parts, received, kept = lax.optimization_barrier((parts, received, kept))

time: 140 us -> 128 us (0.914)
  blocking collectives: 75.6 us -> 57 us
  waiting for transfers between devices: 6.62 us -> 12.7 us
  between operations: 3.73 us -> 1.12 us
  starting transfers between devices: 38 us -> 40.6 us
    psum x1 -> x0, blocking collectives: 18.5 us -> none  [body(): scores = lax.psum(scores, ('near', ANSWER))]
    ppermute x3, waiting for transfers between devices: 0.01 us -> 4.37 us  [body(): incoming.append(lax.ppermute(part, ANSWER, hops) if step else part)]
    ppermute x0 -> x1, starting transfers between devices: none -> 2.74 us  [body(): near_scores = lax.ppermute(own_scores, 'near', [(0, 1), (1, 0)])]
    unnamed x14 -> x10, local copies, waits for them, and re-layouts: 2.78 us -> 1 us
    ppermute x0 -> x1, waiting for transfers between devices: none -> 1.7 us  [body(): near_scores = lax.ppermute(own_scores, 'near', [(0, 1), (1, 0)])]
  transfers between devices with their start and end apart: 7 -> 8, of which waited for: 1 -> 4; matrix products, arithmetic and copies ran while one was open for 2% -> 4% of each run, Pallas kernels for 0% -> 0%
where the time goes in v4:
time: 128 us; the launch traced here: 127 us
  blocking collectives  57 us (45%)
  starting transfers between devices  40.6 us (32%)
  waiting for transfers between devices  12.7 us (10%)
  local copies, waits for them, and re-layouts  7.26 us (6%)
  other arithmetic  4.2 us (3%)
  matrix products  3.96 us (3%)
    all_gather x1, blocking collectives, body(): lax.all_gather(jnp.concatenate([columns, rows, filler]), 'depth', axis=0)  57 us
    all_to_all x1, starting transfers between devices, body(): half = lax.all_to_all(half, 'depth', 0, 0, tiled=True)  15.2 us
    ppermute x3, starting transfers between devices, body(): incoming.append(lax.ppermute(part, ANSWER, hops) if step else part)  10.3 us
    all_to_all x1, starting transfers between devices, body(): parts = lax.all_to_all(parts, ('near', ANSWER), 0, 0, tiled=True)  6.9 us
    ppermute x1, waiting for transfers between devices, body(): received = lax.ppermute(sent, 'near', [(0, 1), (1, 0)])  6.6 us
    ppermute x3, waiting for transfers between devices, body(): incoming.append(lax.ppermute(part, ANSWER, hops) if step else part)  4.37 us
    dot_general x1, matrix products, body(): lax.dot_general(left_rows, weighted.astype(jnp.bfloat16), (((0, 1), (0, 2...  3.96 us
    all_to_all x1, starting transfers between devices, spread(): return lax.all_to_all(copies, axes, 0, 0, tiled=True)  3.58 us
  transfers between devices with their start and end apart: 8, of which 4 were waited for; matrix products, arithmetic and copies ran while one was open for 4% of the time, Pallas kernels for 0%

profile of v4, /device:TPU:6, one launch (start us, length us, event | category | flops | bytes accessed | tf_op | source)
XLA Modules:
  0.0 126.8 jit_solution(1547509111707081855)
XLA Ops:
  0.7 0.9 copy-done
  1.8 0.7 copy.34
  2.5 15.2 %all-to-all-start = ((bf16[16,16,320]{2,1,0:T(8,128)(2,1)}), bf16[16,16,320]{2,1,0:T(8,128)(2,1)S(1)}, u32[]{:S(2)}, u32[]{:S(2)}) async-start(bf16[16,16,320]{2,1,0:T(8,128)(2,1)} %copy.34), calls=%async_computation | async-start | bytes 393216 | tf_op jit(solution)/shard_map/all_to_all | solution.py:47
  17.7 0.9 reduce_sum.43
  18.7 2.7 %collective-permute-start = (f32[128]{0:T(128)S(1)}, f32[128]{0:T(128)S(1)}, u32[]{:S(2)}, u32[]{:S(2)}) collective-permute-start(f32[128]{0:T(128)S(1)} %reduce_sum.43), channel_id=1, source_target_pairs={{0,16},{16,0},{1,17},{17,1},{2,18},{18,2},{3,19},{19,3},{4,20},{20... | collective-permute-start | bytes 1544 | tf_op jit(solution)/shard_map/ppermute | solution.py:53
  22.4 1.7 %collective-permute-done = f32[128]{0:T(128)S(1)} collective-permute-done((f32[128]{0:T(128)S(1)}, f32[128]{0:T(128)S(1)}, u32[]{:S(2)}, u32[]{:S(2)}) %collective-permute-start) | collective-permute-done | bytes 544 | tf_op jit(solution)/shard_map/ppermute | solution.py:53
  24.3 4.9 %collective-permute-start.3 = (bf16[32,888]{1,0:T(8,128)(2,1)S(1)}, bf16[32,888]{1,0:T(8,128)(2,1)S(1)}, u32[]{:S(2)}, u32[]{:S(2)}) collective-permute-start(bf16[32,888]{1,0:T(8,128)(2,1)S(1)} %get-tuple-element.42), channel_id=1, source_target_pairs={{0,3},{1,0},{2,1},{3,2},{4,7},{5,4},{6,5},{7,6},{8,11},{9,8},{10,9... | collective-permute-start | bytes 170504 | tf_op jit(solution)/shard_map/ppermute | solution.py:68
  29.2 2.5 %collective-permute-start.2 = (bf16[32,888]{1,0:T(8,128)(2,1)S(1)}, bf16[32,888]{1,0:T(8,128)(2,1)S(1)}, u32[]{:S(2)}, u32[]{:S(2)}) collective-permute-start(bf16[32,888]{1,0:T(8,128)(2,1)S(1)} %get-tuple-element.41), channel_id=1, source_target_pairs={{0,2},{1,3},{2,0},{3,1},{4,6},{5,7},{6,4},{7,5},{8,10},{9,11},{10,... | collective-permute-start | bytes 170504 | tf_op jit(solution)/shard_map/ppermute | solution.py:68
  31.8 2.9 %collective-permute-start.1 = (bf16[32,888]{1,0:T(8,128)(2,1)S(1)}, bf16[32,888]{1,0:T(8,128)(2,1)S(1)}, u32[]{:S(2)}, u32[]{:S(2)}) collective-permute-start(bf16[32,888]{1,0:T(8,128)(2,1)S(1)} %get-tuple-element.40), channel_id=1, source_target_pairs={{0,1},{1,2},{2,3},{3,0},{4,5},{5,6},{6,7},{7,4},{8,9},{9,10},{10,1... | collective-permute-start | bytes 170504 | tf_op jit(solution)/shard_map/ppermute | solution.py:68
  34.7 2.2 %collective-permute-done.2 = bf16[32,888]{1,0:T(8,128)(2,1)S(1)} collective-permute-done((bf16[32,888]{1,0:T(8,128)(2,1)S(1)}, bf16[32,888]{1,0:T(8,128)(2,1)S(1)}, u32[]{:S(2)}, u32[]{:S(2)}) %collective-permute-start.2) | collective-permute-done | bytes 56864 | tf_op jit(solution)/shard_map/ppermute | solution.py:68
  36.9 2.2 %collective-permute-done.1 = bf16[32,888]{1,0:T(8,128)(2,1)S(1)} collective-permute-done((bf16[32,888]{1,0:T(8,128)(2,1)S(1)}, bf16[32,888]{1,0:T(8,128)(2,1)S(1)}, u32[]{:S(2)}, u32[]{:S(2)}) %collective-permute-start.1) | collective-permute-done | bytes 56864 | tf_op jit(solution)/shard_map/ppermute | solution.py:68
  40.0 1.3 %broadcast_in_dim.37 = bf16[8,16,16,320]{3,2,1,0:T(8,128)(2,1)} broadcast(bf16[16,16,320]{2,1,0:T(8,128)(2,1)S(1)} %all-to-all-done), dimensions={1,2,3} | broadcast | bytes 1474560 | tf_op jit(solution)/shard_map/broadcast_in_dim | solution.py:17
  41.3 3.6 %all-to-all-start.1 = ((bf16[8,16,16,320]{3,2,1,0:T(8,128)(2,1)}), bf16[8,16,16,320]{3,2,1,0:T(8,128)(2,1)S(1)}, u32[]{:S(2)}, u32[]{:S(2)}) async-start(bf16[8,16,16,320]{3,2,1,0:T(8,128)(2,1)} %broadcast_in_dim.37), calls=%async_computation.1 | async-start | bytes 3145728 | tf_op jit(solution)/shard_map/all_to_all | solution.py:18
  44.9 57.0 %all-gather.2 = f16[13952,128]{1,0:T(8,128)(2,1)S(1)} all-gather(f16[872,128]{1,0:T(8,128)(2,1)S(1)} %copy.37), channel_id=2, replica_groups=mesh['depth'=16,'near'=2,'far'=2,'core'=2,'answer'=4] {'depth'}, dimensions={0}, use_global_device_ids=true | all-gather | bytes 3794944 | tf_op jit(solution)/shard_map/all_gather | solution.py:84
  101.9 0.7 multiply_reduce_fusion
  102.6 0.7 broadcast_in_dim.39
  103.3 0.6 broadcast_in_dim.40
  104.3 4.0 %fusion = f32[320,864,1]{1,0,2:T(8,128)S(1)} fusion(bf16[16,128,320]{2,1,0:T(8,128)(2,1)S(1)} %bitcast.69, f16[16,872,128]{2,1,0:T(8,128)(2,1)} %bitcast.65, f32[16,128]{1,0:T(8,128)S(1)} %fusion.9), kind=kOutput, calls=%fused_computation.1 | convolution fusion | flops 1137770496 | bytes 5963776 | tf_op jit(solution)/shard_map/dot_general | solution.py:102
  108.3 1.0 add_convert_fusion
  109.3 6.9 %all-to-all-start.2 = ((bf16[8,40,864]{2,1,0:T(8,128)(2,1)}), bf16[8,40,864]{2,1,0:T(8,128)(2,1)S(1)}, u32[]{:S(2)}, u32[]{:S(2)}) async-start(bf16[8,40,864]{2,1,0:T(8,128)(2,1)} %bitcast.26), calls=%async_computation.2 | async-start | bytes 1146880 | tf_op jit(solution)/shard_map/all_to_all | solution.py:118
  116.2 1.9 %collective-permute-start.4 = (bf16[160,864]{1,0:T(8,128)(2,1)S(1)}, bf16[160,864]{1,0:T(8,128)(2,1)S(1)}, u32[]{:S(2)}, u32[]{:S(2)}) collective-permute-start(bf16[160,864]{1,0:T(8,128)(2,1)S(1)} %dynamic-slice_convert_fusion), channel_id=1, source_target_pairs={{0,16},{16,0},{1,17},{17,1},{2,18},{18,2},{3,19},{19,3},{4,20},{20... | collective-permute-start | bytes 829448 | tf_op jit(solution)/shard_map/ppermute | solution.py:114
  118.1 6.6 %collective-permute-done.4 = bf16[160,864]{1,0:T(8,128)(2,1)S(1)} collective-permute-done((bf16[160,864]{1,0:T(8,128)(2,1)S(1)}, bf16[160,864]{1,0:T(8,128)(2,1)S(1)}, u32[]{:S(2)}, u32[]{:S(2)}) %collective-permute-start.4) | collective-permute-done | bytes 276512 | tf_op jit(solution)/shard_map/ppermute | solution.py:114
  125.0 0.9 reshape.258
  126.0 0.9 convert_add_fusion
  (47 shorter events, 2.7 us)
Async XLA Ops:
  0.6 1.0 copy-start
  0.6 20.9 %copy-start.3 = (bf16[32,3456]{1,0:T(8,128)(2,1)S(1)}, bf16[32,3456]{1,0:T(8,128)(2,1)}, u32[]{:S(2)}) copy-start(bf16[32,3456]{1,0:T(8,128)(2,1)} %param.6) | copy-start | bytes 663556
  2.5 37.5 %all-to-all-start = ((bf16[16,16,320]{2,1,0:T(8,128)(2,1)}), bf16[16,16,320]{2,1,0:T(8,128)(2,1)S(1)}, u32[]{:S(2)}, u32[]{:S(2)}) async-start(bf16[16,16,320]{2,1,0:T(8,128)(2,1)} %copy.34), calls=%async_computation | async-start | bytes 393216 | tf_op jit(solution)/shard_map/all_to_all | solution.py:47
  18.7 5.4 %collective-permute-start = (f32[128]{0:T(128)S(1)}, f32[128]{0:T(128)S(1)}, u32[]{:S(2)}, u32[]{:S(2)}) collective-permute-start(f32[128]{0:T(128)S(1)} %reduce_sum.43), channel_id=1, source_target_pairs={{0,16},{16,0},{1,17},{17,1},{2,18},{18,2},{3,19},{19,3},{4,20},{20... | collective-permute-start | bytes 1544 | tf_op jit(solution)/shard_map/ppermute | solution.py:53
  24.3 10.4 %collective-permute-start.3 = (bf16[32,888]{1,0:T(8,128)(2,1)S(1)}, bf16[32,888]{1,0:T(8,128)(2,1)S(1)}, u32[]{:S(2)}, u32[]{:S(2)}) collective-permute-start(bf16[32,888]{1,0:T(8,128)(2,1)S(1)} %get-tuple-element.42), channel_id=1, source_target_pairs={{0,3},{1,0},{2,1},{3,2},{4,7},{5,4},{6,5},{7,6},{8,11},{9,8},{10,9... | collective-permute-start | bytes 170504 | tf_op jit(solution)/shard_map/ppermute | solution.py:68
  29.2 7.6 %collective-permute-start.2 = (bf16[32,888]{1,0:T(8,128)(2,1)S(1)}, bf16[32,888]{1,0:T(8,128)(2,1)S(1)}, u32[]{:S(2)}, u32[]{:S(2)}) collective-permute-start(bf16[32,888]{1,0:T(8,128)(2,1)S(1)} %get-tuple-element.41), channel_id=1, source_target_pairs={{0,2},{1,3},{2,0},{3,1},{4,6},{5,7},{6,4},{7,5},{8,10},{9,11},{10,... | collective-permute-start | bytes 170504 | tf_op jit(solution)/shard_map/ppermute | solution.py:68
  31.8 7.3 %collective-permute-start.1 = (bf16[32,888]{1,0:T(8,128)(2,1)S(1)}, bf16[32,888]{1,0:T(8,128)(2,1)S(1)}, u32[]{:S(2)}, u32[]{:S(2)}) collective-permute-start(bf16[32,888]{1,0:T(8,128)(2,1)S(1)} %get-tuple-element.40), channel_id=1, source_target_pairs={{0,1},{1,2},{2,3},{3,0},{4,5},{5,6},{6,7},{7,4},{8,9},{9,10},{10,1... | collective-permute-start | bytes 170504 | tf_op jit(solution)/shard_map/ppermute | solution.py:68
  41.3 62.7 %all-to-all-start.1 = ((bf16[8,16,16,320]{3,2,1,0:T(8,128)(2,1)}), bf16[8,16,16,320]{3,2,1,0:T(8,128)(2,1)S(1)}, u32[]{:S(2)}, u32[]{:S(2)}) async-start(bf16[8,16,16,320]{3,2,1,0:T(8,128)(2,1)} %broadcast_in_dim.37), calls=%async_computation.1 | async-start | bytes 3145728 | tf_op jit(solution)/shard_map/all_to_all | solution.py:18
  101.8 2.1 %copy-start.1 = (f16[13952,128]{1,0:T(8,128)(2,1)}, f16[13952,128]{1,0:T(8,128)(2,1)S(1)}, u32[]{:S(2)}) copy-start(f16[13952,128]{1,0:T(8,128)(2,1)S(1)} %all-gather.2) | copy-start | bytes 10715140
  104.3 4.0 %copy-start.2 = (f32[160,864]{1,0:T(8,128)S(1)}, f32[160,864]{1,0:T(8,128)}, u32[]{:S(2)}) copy-start(f32[160,864]{1,0:T(8,128)} %param.4) | copy-start | bytes 1658884
  109.3 15.4 %all-to-all-start.2 = ((bf16[8,40,864]{2,1,0:T(8,128)(2,1)}), bf16[8,40,864]{2,1,0:T(8,128)(2,1)S(1)}, u32[]{:S(2)}, u32[]{:S(2)}) async-start(bf16[8,40,864]{2,1,0:T(8,128)(2,1)} %bitcast.26), calls=%async_computation.2 | async-start | bytes 1146880 | tf_op jit(solution)/shard_map/all_to_all | solution.py:118
  116.2 8.5 %collective-permute-start.4 = (bf16[160,864]{1,0:T(8,128)(2,1)S(1)}, bf16[160,864]{1,0:T(8,128)(2,1)S(1)}, u32[]{:S(2)}, u32[]{:S(2)}) collective-permute-start(bf16[160,864]{1,0:T(8,128)(2,1)S(1)} %dynamic-slice_convert_fusion), channel_id=1, source_target_pairs={{0,16},{16,0},{1,17},{17,1},{2,18},{18,2},{3,19},{19,3},{4,20},{20... | collective-permute-start | bytes 829448 | tf_op jit(solution)/shard_map/ppermute | solution.py:114

commit v5 on v4

--- a/solution.py
+++ b/solution.py
@@ -43,13 +43,13 @@
         left_noise, lax.axis_index("core") * (share // cores), share // cores, 0
     )
     half = half.reshape(share // cores, depth, -1).transpose(1, 0, 2)
-    half, right_noise, returns = lax.optimization_barrier((half, right_noise, returns))
+    own_scores = jnp.sum(returns, axis=1)
+    half, right_noise, own_scores = lax.optimization_barrier((half, right_noise, own_scores))
     half = lax.all_to_all(half, "depth", 0, 0, tiled=True)
     left_rows = spread(half, ("core", ANSWER)).reshape(cores, answers, depth, share // cores, -1)
 
     answer_place = lax.axis_index(ANSWER)
     outgoing = right_noise.reshape(share, answers, tile_cols).transpose(1, 0, 2)
-    own_scores = jnp.sum(returns, axis=1)
     near_scores = lax.ppermute(own_scores, "near", [(0, 1), (1, 0)])
     partial_scores = jnp.where(
         near_place == 0,
@@ -61,16 +61,16 @@
     incoming = []
     for step in range(answers):
         part = lax.dynamic_index_in_dim(
-            outgoing, (answer_place + step) % answers, 0, keepdims=False
+            outgoing, answer_place ^ step, 0, keepdims=False
         )
         part = jnp.concatenate([part, partial_scores], axis=1)
-        hops = [(i, (i + step) % answers) for i in range(answers)]
+        hops = [(i, i ^ step) for i in range(answers)]
         incoming.append(lax.ppermute(part, ANSWER, hops) if step else part)
     incoming = jnp.stack(incoming)
     right_part = jnp.concatenate(
         [
             lax.dynamic_index_in_dim(
-                incoming[..., :tile_cols], (answer_place - i) % answers, 0, keepdims=False
+                incoming[..., :tile_cols], answer_place ^ i, 0, keepdims=False
             )
             for i in range(answers)
         ]
@@ -85,14 +85,10 @@
 
     parts = gathered[:, tile_cols : tile_cols + 3 * near].reshape(depth, 3, near, block)
     all_scores = joined(jnp.moveaxis(parts, 1, 0)) / score_scale
-    total, square_total = lax.optimization_barrier(
-        tuple(
-            jnp.broadcast_to(jnp.sum(value), (1, block))
-            for value in (all_scores, all_scores * all_scores)
-        )
-    )
-    average = total / population
-    variance = square_total / population - average * average
+    totals = jnp.sum(jnp.stack([all_scores, all_scores * all_scores]), axis=(1, 2, 3))
+    totals = lax.optimization_barrier(jnp.broadcast_to(totals[:, None], (2, block)))
+    average = totals[:1] / population
+    variance = totals[1:] / population - average * average
     fitness = lax.dynamic_index_in_dim(all_scores, near_place, 1, keepdims=False)
     fitness = (fitness - average) / jnp.sqrt(variance + 1e-05)
     fitness = fitness / (RIGHT_SCALE * math.sqrt(population))

time: 128 us -> 127 us (level)
    unnamed x10, local copies, waits for them, and re-layouts: 1 us -> 2.51 us
  transfers between devices with their start and end apart: 8 -> 8, of which waited for: 4 -> 4; matrix products, arithmetic and copies ran while one was open for 4% -> 2% of each run, Pallas kernels for 0% -> 0%
where the time goes in v5:
time: 127 us; the launch traced here: 126 us
  blocking collectives  57.1 us (45%)
  starting transfers between devices  40.7 us (32%)
  waiting for transfers between devices  12.1 us (10%)
  local copies, waits for them, and re-layouts  7.51 us (6%)
  matrix products  3.96 us (3%)
  other arithmetic  3.57 us (3%)
    all_gather x1, blocking collectives, body(): lax.all_gather(jnp.concatenate([columns, rows, filler]), 'depth', axis=0)  57.1 us
    all_to_all x1, starting transfers between devices, body(): half = lax.all_to_all(half, 'depth', 0, 0, tiled=True)  15.2 us
    ppermute x3, starting transfers between devices, body(): incoming.append(lax.ppermute(part, ANSWER, hops) if step else part)  9.81 us
    all_to_all x1, starting transfers between devices, body(): parts = lax.all_to_all(parts, ('near', ANSWER), 0, 0, tiled=True)  6.87 us
    ppermute x1, waiting for transfers between devices, body(): received = lax.ppermute(sent, 'near', [(0, 1), (1, 0)])  6.6 us
    all_to_all x1, starting transfers between devices, spread(): return lax.all_to_all(copies, axes, 0, 0, tiled=True)  4.18 us
    dot_general x1, matrix products, body(): lax.dot_general(left_rows, weighted.astype(jnp.bfloat16), (((0, 1), (0, 2...  3.96 us
    ppermute x3, waiting for transfers between devices, body(): incoming.append(lax.ppermute(part, ANSWER, hops) if step else part)  3.68 us
  transfers between devices with their start and end apart: 8, of which 4 were waited for; matrix products, arithmetic and copies ran while one was open for 2% of the time, Pallas kernels for 0%

profile of v5, /device:TPU:6, one launch (start us, length us, event | category | flops | bytes accessed | tf_op | source)
XLA Modules:
  0.0 125.9 jit_solution(16533645855841510048)
XLA Ops:
  0.7 0.9 copy-done
  1.8 0.9 reduce_sum.34
  2.7 0.7 copy.34
  3.5 15.2 %all-to-all-start = ((bf16[16,16,320]{2,1,0:T(8,128)(2,1)}), bf16[16,16,320]{2,1,0:T(8,128)(2,1)S(1)}, u32[]{:S(2)}, u32[]{:S(2)}) async-start(bf16[16,16,320]{2,1,0:T(8,128)(2,1)} %copy.34), calls=%async_computation | async-start | bytes 393216 | tf_op jit(solution)/shard_map/all_to_all | solution.py:48
  18.7 2.7 %collective-permute-start = (f32[128]{0:T(128)S(1)}, f32[128]{0:T(128)S(1)}, u32[]{:S(2)}, u32[]{:S(2)}) collective-permute-start(f32[128]{0:T(128)S(1)} %reduce_sum.34), channel_id=1, source_target_pairs={{0,16},{16,0},{1,17},{17,1},{2,18},{18,2},{3,19},{19,3},{4,20},{20... | collective-permute-start | bytes 1544 | tf_op jit(solution)/shard_map/ppermute | solution.py:53
  21.7 0.5 constant_dynamic-slice_fusion.3
  22.3 1.8 %collective-permute-done = f32[128]{0:T(128)S(1)} collective-permute-done((f32[128]{0:T(128)S(1)}, f32[128]{0:T(128)S(1)}, u32[]{:S(2)}, u32[]{:S(2)}) %collective-permute-start) | collective-permute-done | bytes 544 | tf_op jit(solution)/shard_map/ppermute | solution.py:53
  24.3 4.9 %collective-permute-start.3 = (bf16[32,888]{1,0:T(8,128)(2,1)S(1)}, bf16[32,888]{1,0:T(8,128)(2,1)S(1)}, u32[]{:S(2)}, u32[]{:S(2)}) collective-permute-start(bf16[32,888]{1,0:T(8,128)(2,1)S(1)} %get-tuple-element.37), channel_id=1, source_target_pairs={{0,3},{1,2},{2,1},{3,0},{4,7},{5,6},{6,5},{7,4},{8,11},{9,10},{10,... | collective-permute-start | bytes 170504 | tf_op jit(solution)/shard_map/ppermute | solution.py:68
  29.3 2.5 %collective-permute-start.2 = (bf16[32,888]{1,0:T(8,128)(2,1)S(1)}, bf16[32,888]{1,0:T(8,128)(2,1)S(1)}, u32[]{:S(2)}, u32[]{:S(2)}) collective-permute-start(bf16[32,888]{1,0:T(8,128)(2,1)S(1)} %get-tuple-element.36), channel_id=1, source_target_pairs={{0,2},{1,3},{2,0},{3,1},{4,6},{5,7},{6,4},{7,5},{8,10},{9,11},{10,... | collective-permute-start | bytes 170504 | tf_op jit(solution)/shard_map/ppermute | solution.py:68
  31.8 2.4 %collective-permute-start.1 = (bf16[32,888]{1,0:T(8,128)(2,1)S(1)}, bf16[32,888]{1,0:T(8,128)(2,1)S(1)}, u32[]{:S(2)}, u32[]{:S(2)}) collective-permute-start(bf16[32,888]{1,0:T(8,128)(2,1)S(1)} %get-tuple-element.35), channel_id=1, source_target_pairs={{0,1},{1,0},{2,3},{3,2},{4,5},{5,4},{6,7},{7,6},{8,9},{9,8},{10,11... | collective-permute-start | bytes 170504 | tf_op jit(solution)/shard_map/ppermute | solution.py:68
  34.2 2.8 %collective-permute-done.2 = bf16[32,888]{1,0:T(8,128)(2,1)S(1)} collective-permute-done((bf16[32,888]{1,0:T(8,128)(2,1)S(1)}, bf16[32,888]{1,0:T(8,128)(2,1)S(1)}, u32[]{:S(2)}, u32[]{:S(2)}) %collective-permute-start.2) | collective-permute-done | bytes 56864 | tf_op jit(solution)/shard_map/ppermute | solution.py:68
  37.0 0.9 collective-permute-done.1
  38.5 0.3 copy.37
  38.8 1.3 %broadcast_in_dim.37 = bf16[8,16,16,320]{3,2,1,0:T(8,128)(2,1)} broadcast(bf16[16,16,320]{2,1,0:T(8,128)(2,1)S(1)} %all-to-all-done), dimensions={1,2,3} | broadcast | bytes 1474560 | tf_op jit(solution)/shard_map/broadcast_in_dim | solution.py:17
  40.1 4.2 %all-to-all-start.1 = ((bf16[8,16,16,320]{3,2,1,0:T(8,128)(2,1)}), bf16[8,16,16,320]{3,2,1,0:T(8,128)(2,1)S(1)}, u32[]{:S(2)}, u32[]{:S(2)}) async-start(bf16[8,16,16,320]{3,2,1,0:T(8,128)(2,1)} %broadcast_in_dim.37), calls=%async_computation.1 | async-start | bytes 3145728 | tf_op jit(solution)/shard_map/all_to_all | solution.py:18
  44.2 57.1 %all-gather.2 = f16[13952,128]{1,0:T(8,128)(2,1)S(1)} all-gather(f16[872,128]{1,0:T(8,128)(2,1)S(1)} %copy.37), channel_id=2, replica_groups=mesh['depth'=16,'near'=2,'far'=2,'core'=2,'answer'=4] {'depth'}, dimensions={0}, use_global_device_ids=true | all-gather | bytes 3794944 | tf_op jit(solution)/shard_map/all_gather | solution.py:84
  101.6 1.5 %copy-done.1 = f16[13952,128]{1,0:T(8,128)(2,1)} copy-done((f16[13952,128]{1,0:T(8,128)(2,1)}, f16[13952,128]{1,0:T(8,128)(2,1)S(1)}, u32[]{:S(2)}) %copy-start.1) | copy-done | bytes 3571736
  103.3 4.0 %fusion = f32[320,864,1]{1,0,2:T(8,128)S(1)} fusion(bf16[16,128,320]{2,1,0:T(8,128)(2,1)S(1)} %bitcast.69, f16[16,872,128]{2,1,0:T(8,128)(2,1)} %bitcast.65, f32[16,128]{1,0:T(8,128)S(1)} %fusion.9), kind=kOutput, calls=%fused_computation.1 | convolution fusion | flops 1137770496 | bytes 5963776 | tf_op jit(solution)/shard_map/dot_general | solution.py:98
  107.4 1.0 add_convert_fusion
  108.4 6.9 %all-to-all-start.2 = ((bf16[8,40,864]{2,1,0:T(8,128)(2,1)}), bf16[8,40,864]{2,1,0:T(8,128)(2,1)S(1)}, u32[]{:S(2)}, u32[]{:S(2)}) async-start(bf16[8,40,864]{2,1,0:T(8,128)(2,1)} %bitcast.26), calls=%async_computation.2 | async-start | bytes 1146880 | tf_op jit(solution)/shard_map/all_to_all | solution.py:114
  115.3 1.9 %collective-permute-start.4 = (bf16[160,864]{1,0:T(8,128)(2,1)S(1)}, bf16[160,864]{1,0:T(8,128)(2,1)S(1)}, u32[]{:S(2)}, u32[]{:S(2)}) collective-permute-start(bf16[160,864]{1,0:T(8,128)(2,1)S(1)} %dynamic-slice_convert_fusion), channel_id=1, source_target_pairs={{0,16},{16,0},{1,17},{17,1},{2,18},{18,2},{3,19},{19,3},{4,20},{20... | collective-permute-start | bytes 829448 | tf_op jit(solution)/shard_map/ppermute | solution.py:110
  117.2 6.6 %collective-permute-done.4 = bf16[160,864]{1,0:T(8,128)(2,1)S(1)} collective-permute-done((bf16[160,864]{1,0:T(8,128)(2,1)S(1)}, bf16[160,864]{1,0:T(8,128)(2,1)S(1)}, u32[]{:S(2)}, u32[]{:S(2)}) %collective-permute-start.4) | collective-permute-done | bytes 276512 | tf_op jit(solution)/shard_map/ppermute | solution.py:110
  124.1 0.9 reshape.259
  125.0 0.9 convert_add_fusion
  (47 shorter events, 2.2 us)
Async XLA Ops:
  0.6 1.0 copy-start
  0.6 20.8 %copy-start.3 = (bf16[32,3456]{1,0:T(8,128)(2,1)S(1)}, bf16[32,3456]{1,0:T(8,128)(2,1)}, u32[]{:S(2)}) copy-start(bf16[32,3456]{1,0:T(8,128)(2,1)} %param.6) | copy-start | bytes 663556
  3.5 35.3 %all-to-all-start = ((bf16[16,16,320]{2,1,0:T(8,128)(2,1)}), bf16[16,16,320]{2,1,0:T(8,128)(2,1)S(1)}, u32[]{:S(2)}, u32[]{:S(2)}) async-start(bf16[16,16,320]{2,1,0:T(8,128)(2,1)} %copy.34), calls=%async_computation | async-start | bytes 393216 | tf_op jit(solution)/shard_map/all_to_all | solution.py:48
  18.7 5.4 %collective-permute-start = (f32[128]{0:T(128)S(1)}, f32[128]{0:T(128)S(1)}, u32[]{:S(2)}, u32[]{:S(2)}) collective-permute-start(f32[128]{0:T(128)S(1)} %reduce_sum.34), channel_id=1, source_target_pairs={{0,16},{16,0},{1,17},{17,1},{2,18},{18,2},{3,19},{19,3},{4,20},{20... | collective-permute-start | bytes 1544 | tf_op jit(solution)/shard_map/ppermute | solution.py:53
  24.3 9.8 %collective-permute-start.3 = (bf16[32,888]{1,0:T(8,128)(2,1)S(1)}, bf16[32,888]{1,0:T(8,128)(2,1)S(1)}, u32[]{:S(2)}, u32[]{:S(2)}) collective-permute-start(bf16[32,888]{1,0:T(8,128)(2,1)S(1)} %get-tuple-element.37), channel_id=1, source_target_pairs={{0,3},{1,2},{2,1},{3,0},{4,7},{5,6},{6,5},{7,4},{8,11},{9,10},{10,... | collective-permute-start | bytes 170504 | tf_op jit(solution)/shard_map/ppermute | solution.py:68
  29.3 7.7 %collective-permute-start.2 = (bf16[32,888]{1,0:T(8,128)(2,1)S(1)}, bf16[32,888]{1,0:T(8,128)(2,1)S(1)}, u32[]{:S(2)}, u32[]{:S(2)}) collective-permute-start(bf16[32,888]{1,0:T(8,128)(2,1)S(1)} %get-tuple-element.36), channel_id=1, source_target_pairs={{0,2},{1,3},{2,0},{3,1},{4,6},{5,7},{6,4},{7,5},{8,10},{9,11},{10,... | collective-permute-start | bytes 170504 | tf_op jit(solution)/shard_map/ppermute | solution.py:68
  31.8 6.1 %collective-permute-start.1 = (bf16[32,888]{1,0:T(8,128)(2,1)S(1)}, bf16[32,888]{1,0:T(8,128)(2,1)S(1)}, u32[]{:S(2)}, u32[]{:S(2)}) collective-permute-start(bf16[32,888]{1,0:T(8,128)(2,1)S(1)} %get-tuple-element.35), channel_id=1, source_target_pairs={{0,1},{1,0},{2,3},{3,2},{4,5},{5,4},{6,7},{7,6},{8,9},{9,8},{10,11... | collective-permute-start | bytes 170504 | tf_op jit(solution)/shard_map/ppermute | solution.py:68
  40.1 63.0 %all-to-all-start.1 = ((bf16[8,16,16,320]{3,2,1,0:T(8,128)(2,1)}), bf16[8,16,16,320]{3,2,1,0:T(8,128)(2,1)S(1)}, u32[]{:S(2)}, u32[]{:S(2)}) async-start(bf16[8,16,16,320]{3,2,1,0:T(8,128)(2,1)} %broadcast_in_dim.37), calls=%async_computation.1 | async-start | bytes 3145728 | tf_op jit(solution)/shard_map/all_to_all | solution.py:18
  101.3 1.8 %copy-start.1 = (f16[13952,128]{1,0:T(8,128)(2,1)}, f16[13952,128]{1,0:T(8,128)(2,1)S(1)}, u32[]{:S(2)}) copy-start(f16[13952,128]{1,0:T(8,128)(2,1)S(1)} %all-gather.2) | copy-start | bytes 10715140
  103.3 4.0 %copy-start.2 = (f32[160,864]{1,0:T(8,128)S(1)}, f32[160,864]{1,0:T(8,128)}, u32[]{:S(2)}) copy-start(f32[160,864]{1,0:T(8,128)} %param.4) | copy-start | bytes 1658884
  108.4 15.4 %all-to-all-start.2 = ((bf16[8,40,864]{2,1,0:T(8,128)(2,1)}), bf16[8,40,864]{2,1,0:T(8,128)(2,1)S(1)}, u32[]{:S(2)}, u32[]{:S(2)}) async-start(bf16[8,40,864]{2,1,0:T(8,128)(2,1)} %bitcast.26), calls=%async_computation.2 | async-start | bytes 1146880 | tf_op jit(solution)/shard_map/all_to_all | solution.py:114
  115.3 8.5 %collective-permute-start.4 = (bf16[160,864]{1,0:T(8,128)(2,1)S(1)}, bf16[160,864]{1,0:T(8,128)(2,1)S(1)}, u32[]{:S(2)}, u32[]{:S(2)}) collective-permute-start(bf16[160,864]{1,0:T(8,128)(2,1)S(1)} %dynamic-slice_convert_fusion), channel_id=1, source_target_pairs={{0,16},{16,0},{1,17},{17,1},{2,18},{18,2},{3,19},{19,3},{4,20},{20... | collective-permute-start | bytes 829448 | tf_op jit(solution)/shard_map/ppermute | solution.py:110

commit v6 on v5

--- a/solution.py
+++ b/solution.py
@@ -112,11 +112,11 @@
     parts, kept = lax.optimization_barrier((parts.astype(jnp.bfloat16), master + kept))
     parts = parts.reshape(near * answers, -1, tile_cols)
     parts = lax.all_to_all(parts, ("near", ANSWER), 0, 0, tiled=True)
-    parts, received, kept = lax.optimization_barrier((parts, received, kept))
-    new_master = kept + received.astype(jnp.float32)
     parts = parts.reshape(near, answers, -1, tile_cols).astype(jnp.float32)
     rollout = (parts[0] + parts[1]).astype(jnp.bfloat16)
     rollout = rollout.transpose(1, 0, 2).reshape(-1, answers * tile_cols)
+    rollout, received, kept = lax.optimization_barrier((rollout, received, kept))
+    new_master = kept + received.astype(jnp.float32)
     return (new_master, rollout)
 
 

time: 127 us -> 126 us (level)
    ppermute x1, waiting for transfers between devices: 6.6 us -> 0.01 us  [body(): received = lax.ppermute(sent, 'near', [(0, 1), (1, 0)])]
    all_to_all x1, waiting for transfers between devices: 0.01 us -> 5.58 us  [body(): parts = lax.all_to_all(parts, ('near', ANSWER), 0, 0, tiled=True)]
  transfers between devices with their start and end apart: 8 -> 8, of which waited for: 4 -> 4; matrix products, arithmetic and copies ran while one was open for 2% -> 3% of each run, Pallas kernels for 0% -> 0%
where the time goes in v6:
time: 126 us; the launch traced here: 125 us
  blocking collectives  57.1 us (45%)
  starting transfers between devices  40.7 us (32%)
  waiting for transfers between devices  11.1 us (9%)
  local copies, waits for them, and re-layouts  7.51 us (6%)
  matrix products  3.96 us (3%)
  other arithmetic  3.57 us (3%)
    all_gather x1, blocking collectives, body(): lax.all_gather(jnp.concatenate([columns, rows, filler]), 'depth', axis=0)  57.1 us
    all_to_all x1, starting transfers between devices, body(): half = lax.all_to_all(half, 'depth', 0, 0, tiled=True)  15.2 us
    ppermute x3, starting transfers between devices, body(): incoming.append(lax.ppermute(part, ANSWER, hops) if step else part)  9.81 us
    all_to_all x1, starting transfers between devices, body(): parts = lax.all_to_all(parts, ('near', ANSWER), 0, 0, tiled=True)  6.87 us
    all_to_all x1, waiting for transfers between devices, body(): parts = lax.all_to_all(parts, ('near', ANSWER), 0, 0, tiled=True)  5.58 us
    all_to_all x1, starting transfers between devices, spread(): return lax.all_to_all(copies, axes, 0, 0, tiled=True)  4.18 us
    dot_general x1, matrix products, body(): lax.dot_general(left_rows, weighted.astype(jnp.bfloat16), (((0, 1), (0, 2...  3.96 us
    ppermute x3, waiting for transfers between devices, body(): incoming.append(lax.ppermute(part, ANSWER, hops) if step else part)  3.68 us
  transfers between devices with their start and end apart: 8, of which 4 were waited for; matrix products, arithmetic and copies ran while one was open for 3% of the time, Pallas kernels for 0%

profile of v6, /device:TPU:6, one launch (start us, length us, event | category | flops | bytes accessed | tf_op | source)
XLA Modules:
  0.0 124.9 jit_solution(8035559563952194478)
XLA Ops:
  0.7 0.9 copy-done
  1.8 0.9 reduce_sum.34
  2.7 0.7 copy.34
  3.5 15.2 %all-to-all-start = ((bf16[16,16,320]{2,1,0:T(8,128)(2,1)}), bf16[16,16,320]{2,1,0:T(8,128)(2,1)S(1)}, u32[]{:S(2)}, u32[]{:S(2)}) async-start(bf16[16,16,320]{2,1,0:T(8,128)(2,1)} %copy.34), calls=%async_computation | async-start | bytes 393216 | tf_op jit(solution)/shard_map/all_to_all | solution.py:48
  18.7 2.7 %collective-permute-start = (f32[128]{0:T(128)S(1)}, f32[128]{0:T(128)S(1)}, u32[]{:S(2)}, u32[]{:S(2)}) collective-permute-start(f32[128]{0:T(128)S(1)} %reduce_sum.34), channel_id=1, source_target_pairs={{0,16},{16,0},{1,17},{17,1},{2,18},{18,2},{3,19},{19,3},{4,20},{20... | collective-permute-start | bytes 1544 | tf_op jit(solution)/shard_map/ppermute | solution.py:53
  21.7 0.5 constant_dynamic-slice_fusion.3
  22.3 1.8 %collective-permute-done = f32[128]{0:T(128)S(1)} collective-permute-done((f32[128]{0:T(128)S(1)}, f32[128]{0:T(128)S(1)}, u32[]{:S(2)}, u32[]{:S(2)}) %collective-permute-start) | collective-permute-done | bytes 544 | tf_op jit(solution)/shard_map/ppermute | solution.py:53
  24.3 4.9 %collective-permute-start.3 = (bf16[32,888]{1,0:T(8,128)(2,1)S(1)}, bf16[32,888]{1,0:T(8,128)(2,1)S(1)}, u32[]{:S(2)}, u32[]{:S(2)}) collective-permute-start(bf16[32,888]{1,0:T(8,128)(2,1)S(1)} %get-tuple-element.37), channel_id=1, source_target_pairs={{0,3},{1,2},{2,1},{3,0},{4,7},{5,6},{6,5},{7,4},{8,11},{9,10},{10,... | collective-permute-start | bytes 170504 | tf_op jit(solution)/shard_map/ppermute | solution.py:68
  29.3 2.5 %collective-permute-start.2 = (bf16[32,888]{1,0:T(8,128)(2,1)S(1)}, bf16[32,888]{1,0:T(8,128)(2,1)S(1)}, u32[]{:S(2)}, u32[]{:S(2)}) collective-permute-start(bf16[32,888]{1,0:T(8,128)(2,1)S(1)} %get-tuple-element.36), channel_id=1, source_target_pairs={{0,2},{1,3},{2,0},{3,1},{4,6},{5,7},{6,4},{7,5},{8,10},{9,11},{10,... | collective-permute-start | bytes 170504 | tf_op jit(solution)/shard_map/ppermute | solution.py:68
  31.8 2.4 %collective-permute-start.1 = (bf16[32,888]{1,0:T(8,128)(2,1)S(1)}, bf16[32,888]{1,0:T(8,128)(2,1)S(1)}, u32[]{:S(2)}, u32[]{:S(2)}) collective-permute-start(bf16[32,888]{1,0:T(8,128)(2,1)S(1)} %get-tuple-element.35), channel_id=1, source_target_pairs={{0,1},{1,0},{2,3},{3,2},{4,5},{5,4},{6,7},{7,6},{8,9},{9,8},{10,11... | collective-permute-start | bytes 170504 | tf_op jit(solution)/shard_map/ppermute | solution.py:68
  34.2 2.8 %collective-permute-done.2 = bf16[32,888]{1,0:T(8,128)(2,1)S(1)} collective-permute-done((bf16[32,888]{1,0:T(8,128)(2,1)S(1)}, bf16[32,888]{1,0:T(8,128)(2,1)S(1)}, u32[]{:S(2)}, u32[]{:S(2)}) %collective-permute-start.2) | collective-permute-done | bytes 56864 | tf_op jit(solution)/shard_map/ppermute | solution.py:68
  37.0 0.9 collective-permute-done.1
  38.5 0.3 copy.37
  38.8 1.3 %broadcast_in_dim.37 = bf16[8,16,16,320]{3,2,1,0:T(8,128)(2,1)} broadcast(bf16[16,16,320]{2,1,0:T(8,128)(2,1)S(1)} %all-to-all-done), dimensions={1,2,3} | broadcast | bytes 1474560 | tf_op jit(solution)/shard_map/broadcast_in_dim | solution.py:17
  40.1 4.2 %all-to-all-start.1 = ((bf16[8,16,16,320]{3,2,1,0:T(8,128)(2,1)}), bf16[8,16,16,320]{3,2,1,0:T(8,128)(2,1)S(1)}, u32[]{:S(2)}, u32[]{:S(2)}) async-start(bf16[8,16,16,320]{3,2,1,0:T(8,128)(2,1)} %broadcast_in_dim.37), calls=%async_computation.1 | async-start | bytes 3145728 | tf_op jit(solution)/shard_map/all_to_all | solution.py:18
  44.2 57.1 %all-gather.2 = f16[13952,128]{1,0:T(8,128)(2,1)S(1)} all-gather(f16[872,128]{1,0:T(8,128)(2,1)S(1)} %copy.37), channel_id=2, replica_groups=mesh['depth'=16,'near'=2,'far'=2,'core'=2,'answer'=4] {'depth'}, dimensions={0}, use_global_device_ids=true | all-gather | bytes 3794944 | tf_op jit(solution)/shard_map/all_gather | solution.py:84
  101.6 1.5 %copy-done.1 = f16[13952,128]{1,0:T(8,128)(2,1)} copy-done((f16[13952,128]{1,0:T(8,128)(2,1)}, f16[13952,128]{1,0:T(8,128)(2,1)S(1)}, u32[]{:S(2)}) %copy-start.1) | copy-done | bytes 3571736
  103.3 4.0 %fusion = f32[320,864,1]{1,0,2:T(8,128)S(1)} fusion(bf16[16,128,320]{2,1,0:T(8,128)(2,1)S(1)} %bitcast.69, f16[16,872,128]{2,1,0:T(8,128)(2,1)} %bitcast.65, f32[16,128]{1,0:T(8,128)S(1)} %fusion.9), kind=kOutput, calls=%fused_computation.1 | convolution fusion | flops 1137770496 | bytes 5963776 | tf_op jit(solution)/shard_map/dot_general | solution.py:98
  107.4 1.0 add_convert_fusion
  108.4 6.9 %all-to-all-start.2 = ((bf16[8,40,864]{2,1,0:T(8,128)(2,1)}), bf16[8,40,864]{2,1,0:T(8,128)(2,1)S(1)}, u32[]{:S(2)}, u32[]{:S(2)}) async-start(bf16[8,40,864]{2,1,0:T(8,128)(2,1)} %bitcast.26), calls=%async_computation.2 | async-start | bytes 1146880 | tf_op jit(solution)/shard_map/all_to_all | solution.py:114
  115.3 1.9 %collective-permute-start.4 = (bf16[160,864]{1,0:T(8,128)(2,1)S(1)}, bf16[160,864]{1,0:T(8,128)(2,1)S(1)}, u32[]{:S(2)}, u32[]{:S(2)}) collective-permute-start(bf16[160,864]{1,0:T(8,128)(2,1)S(1)} %dynamic-slice_convert_fusion), channel_id=1, source_target_pairs={{0,16},{16,0},{1,17},{17,1},{2,18},{18,2},{3,19},{19,3},{4,20},{20... | collective-permute-start | bytes 829448 | tf_op jit(solution)/shard_map/ppermute | solution.py:110
  117.2 5.6 %all-to-all-done.2 = bf16[8,40,864]{2,1,0:T(8,128)(2,1)S(1)} async-done(((bf16[8,40,864]{2,1,0:T(8,128)(2,1)}), bf16[8,40,864]{2,1,0:T(8,128)(2,1)S(1)}, u32[]{:S(2)}, u32[]{:S(2)}) %all-to-all-start.2) | async-done | bytes 552992 | tf_op jit(solution)/shard_map/all_to_all | solution.py:114
  123.0 0.9 reshape.259
  124.0 0.9 convert_add_fusion
  (47 shorter events, 2.2 us)
Async XLA Ops:
  0.6 1.0 copy-start
  0.6 20.8 %copy-start.3 = (bf16[32,3456]{1,0:T(8,128)(2,1)S(1)}, bf16[32,3456]{1,0:T(8,128)(2,1)}, u32[]{:S(2)}) copy-start(bf16[32,3456]{1,0:T(8,128)(2,1)} %param.6) | copy-start | bytes 663556
  3.5 35.3 %all-to-all-start = ((bf16[16,16,320]{2,1,0:T(8,128)(2,1)}), bf16[16,16,320]{2,1,0:T(8,128)(2,1)S(1)}, u32[]{:S(2)}, u32[]{:S(2)}) async-start(bf16[16,16,320]{2,1,0:T(8,128)(2,1)} %copy.34), calls=%async_computation | async-start | bytes 393216 | tf_op jit(solution)/shard_map/all_to_all | solution.py:48
  18.7 5.4 %collective-permute-start = (f32[128]{0:T(128)S(1)}, f32[128]{0:T(128)S(1)}, u32[]{:S(2)}, u32[]{:S(2)}) collective-permute-start(f32[128]{0:T(128)S(1)} %reduce_sum.34), channel_id=1, source_target_pairs={{0,16},{16,0},{1,17},{17,1},{2,18},{18,2},{3,19},{19,3},{4,20},{20... | collective-permute-start | bytes 1544 | tf_op jit(solution)/shard_map/ppermute | solution.py:53
  24.3 9.8 %collective-permute-start.3 = (bf16[32,888]{1,0:T(8,128)(2,1)S(1)}, bf16[32,888]{1,0:T(8,128)(2,1)S(1)}, u32[]{:S(2)}, u32[]{:S(2)}) collective-permute-start(bf16[32,888]{1,0:T(8,128)(2,1)S(1)} %get-tuple-element.37), channel_id=1, source_target_pairs={{0,3},{1,2},{2,1},{3,0},{4,7},{5,6},{6,5},{7,4},{8,11},{9,10},{10,... | collective-permute-start | bytes 170504 | tf_op jit(solution)/shard_map/ppermute | solution.py:68
  29.3 7.7 %collective-permute-start.2 = (bf16[32,888]{1,0:T(8,128)(2,1)S(1)}, bf16[32,888]{1,0:T(8,128)(2,1)S(1)}, u32[]{:S(2)}, u32[]{:S(2)}) collective-permute-start(bf16[32,888]{1,0:T(8,128)(2,1)S(1)} %get-tuple-element.36), channel_id=1, source_target_pairs={{0,2},{1,3},{2,0},{3,1},{4,6},{5,7},{6,4},{7,5},{8,10},{9,11},{10,... | collective-permute-start | bytes 170504 | tf_op jit(solution)/shard_map/ppermute | solution.py:68
  31.8 6.1 %collective-permute-start.1 = (bf16[32,888]{1,0:T(8,128)(2,1)S(1)}, bf16[32,888]{1,0:T(8,128)(2,1)S(1)}, u32[]{:S(2)}, u32[]{:S(2)}) collective-permute-start(bf16[32,888]{1,0:T(8,128)(2,1)S(1)} %get-tuple-element.35), channel_id=1, source_target_pairs={{0,1},{1,0},{2,3},{3,2},{4,5},{5,4},{6,7},{7,6},{8,9},{9,8},{10,11... | collective-permute-start | bytes 170504 | tf_op jit(solution)/shard_map/ppermute | solution.py:68
  40.1 63.0 %all-to-all-start.1 = ((bf16[8,16,16,320]{3,2,1,0:T(8,128)(2,1)}), bf16[8,16,16,320]{3,2,1,0:T(8,128)(2,1)S(1)}, u32[]{:S(2)}, u32[]{:S(2)}) async-start(bf16[8,16,16,320]{3,2,1,0:T(8,128)(2,1)} %broadcast_in_dim.37), calls=%async_computation.1 | async-start | bytes 3145728 | tf_op jit(solution)/shard_map/all_to_all | solution.py:18
  101.3 1.8 %copy-start.1 = (f16[13952,128]{1,0:T(8,128)(2,1)}, f16[13952,128]{1,0:T(8,128)(2,1)S(1)}, u32[]{:S(2)}) copy-start(f16[13952,128]{1,0:T(8,128)(2,1)S(1)} %all-gather.2) | copy-start | bytes 10715140
  103.3 4.0 %copy-start.2 = (f32[160,864]{1,0:T(8,128)S(1)}, f32[160,864]{1,0:T(8,128)}, u32[]{:S(2)}) copy-start(f32[160,864]{1,0:T(8,128)} %param.4) | copy-start | bytes 1658884
  108.4 14.4 %all-to-all-start.2 = ((bf16[8,40,864]{2,1,0:T(8,128)(2,1)}), bf16[8,40,864]{2,1,0:T(8,128)(2,1)S(1)}, u32[]{:S(2)}, u32[]{:S(2)}) async-start(bf16[8,40,864]{2,1,0:T(8,128)(2,1)} %bitcast.26), calls=%async_computation.2 | async-start | bytes 1146880 | tf_op jit(solution)/shard_map/all_to_all | solution.py:114
  115.3 8.7 %collective-permute-start.4 = (bf16[160,864]{1,0:T(8,128)(2,1)S(1)}, bf16[160,864]{1,0:T(8,128)(2,1)S(1)}, u32[]{:S(2)}, u32[]{:S(2)}) collective-permute-start(bf16[160,864]{1,0:T(8,128)(2,1)S(1)} %dynamic-slice_convert_fusion), channel_id=1, source_target_pairs={{0,16},{16,0},{1,17},{17,1},{2,18},{18,2},{3,19},{19,3},{4,20},{20... | collective-permute-start | bytes 829448 | tf_op jit(solution)/shard_map/ppermute | solution.py:110

commit v7 on v6

--- a/solution.py
+++ b/solution.py
@@ -44,7 +44,7 @@
     )
     half = half.reshape(share // cores, depth, -1).transpose(1, 0, 2)
     own_scores = jnp.sum(returns, axis=1)
-    half, right_noise, own_scores = lax.optimization_barrier((half, right_noise, own_scores))
+    half, own_scores = lax.optimization_barrier((half, own_scores))
     half = lax.all_to_all(half, "depth", 0, 0, tiled=True)
     left_rows = spread(half, ("core", ANSWER)).reshape(cores, answers, depth, share // cores, -1)
 

time: 126 us -> 126 us (level)
  no operation moved by 1% of the time
where the time goes in v7:
time: 126 us; the launch traced here: 125 us
  blocking collectives  57.1 us (45%)
  starting transfers between devices  40.7 us (32%)
  waiting for transfers between devices  11.1 us (9%)
  local copies, waits for them, and re-layouts  7.51 us (6%)
  matrix products  3.96 us (3%)
  other arithmetic  3.57 us (3%)
    all_gather x1, blocking collectives, body(): lax.all_gather(jnp.concatenate([columns, rows, filler]), 'depth', axis=0)  57.1 us
    all_to_all x1, starting transfers between devices, body(): half = lax.all_to_all(half, 'depth', 0, 0, tiled=True)  15.2 us
    ppermute x3, starting transfers between devices, body(): incoming.append(lax.ppermute(part, ANSWER, hops) if step else part)  9.81 us
    all_to_all x1, starting transfers between devices, body(): parts = lax.all_to_all(parts, ('near', ANSWER), 0, 0, tiled=True)  6.87 us
    all_to_all x1, waiting for transfers between devices, body(): parts = lax.all_to_all(parts, ('near', ANSWER), 0, 0, tiled=True)  5.58 us
    all_to_all x1, starting transfers between devices, spread(): return lax.all_to_all(copies, axes, 0, 0, tiled=True)  4.18 us
    dot_general x1, matrix products, body(): lax.dot_general(left_rows, weighted.astype(jnp.bfloat16), (((0, 1), (0, 2...  3.96 us
    ppermute x3, waiting for transfers between devices, body(): incoming.append(lax.ppermute(part, ANSWER, hops) if step else part)  3.68 us
  transfers between devices with their start and end apart: 8, of which 4 were waited for; matrix products, arithmetic and copies ran while one was open for 3% of the time, Pallas kernels for 0%

profile of v7, /device:TPU:6, one launch (start us, length us, event | category | flops | bytes accessed | tf_op | source)
XLA Modules:
  0.0 124.9 jit_solution(8035559563952194478)
XLA Ops:
  0.7 0.9 copy-done
  1.8 0.9 reduce_sum.34
  2.7 0.7 copy.34
  3.5 15.2 %all-to-all-start = ((bf16[16,16,320]{2,1,0:T(8,128)(2,1)}), bf16[16,16,320]{2,1,0:T(8,128)(2,1)S(1)}, u32[]{:S(2)}, u32[]{:S(2)}) async-start(bf16[16,16,320]{2,1,0:T(8,128)(2,1)} %copy.34), calls=%async_computation | async-start | bytes 393216 | tf_op jit(solution)/shard_map/all_to_all | solution.py:48
  18.7 2.7 %collective-permute-start = (f32[128]{0:T(128)S(1)}, f32[128]{0:T(128)S(1)}, u32[]{:S(2)}, u32[]{:S(2)}) collective-permute-start(f32[128]{0:T(128)S(1)} %reduce_sum.34), channel_id=1, source_target_pairs={{0,16},{16,0},{1,17},{17,1},{2,18},{18,2},{3,19},{19,3},{4,20},{20... | collective-permute-start | bytes 1544 | tf_op jit(solution)/shard_map/ppermute | solution.py:53
  21.7 0.5 constant_dynamic-slice_fusion.3
  22.3 1.8 %collective-permute-done = f32[128]{0:T(128)S(1)} collective-permute-done((f32[128]{0:T(128)S(1)}, f32[128]{0:T(128)S(1)}, u32[]{:S(2)}, u32[]{:S(2)}) %collective-permute-start) | collective-permute-done | bytes 544 | tf_op jit(solution)/shard_map/ppermute | solution.py:53
  24.3 4.9 %collective-permute-start.3 = (bf16[32,888]{1,0:T(8,128)(2,1)S(1)}, bf16[32,888]{1,0:T(8,128)(2,1)S(1)}, u32[]{:S(2)}, u32[]{:S(2)}) collective-permute-start(bf16[32,888]{1,0:T(8,128)(2,1)S(1)} %get-tuple-element.35), channel_id=1, source_target_pairs={{0,3},{1,2},{2,1},{3,0},{4,7},{5,6},{6,5},{7,4},{8,11},{9,10},{10,... | collective-permute-start | bytes 170504 | tf_op jit(solution)/shard_map/ppermute | solution.py:68
  29.3 2.5 %collective-permute-start.2 = (bf16[32,888]{1,0:T(8,128)(2,1)S(1)}, bf16[32,888]{1,0:T(8,128)(2,1)S(1)}, u32[]{:S(2)}, u32[]{:S(2)}) collective-permute-start(bf16[32,888]{1,0:T(8,128)(2,1)S(1)} %get-tuple-element.34), channel_id=1, source_target_pairs={{0,2},{1,3},{2,0},{3,1},{4,6},{5,7},{6,4},{7,5},{8,10},{9,11},{10,... | collective-permute-start | bytes 170504 | tf_op jit(solution)/shard_map/ppermute | solution.py:68
  31.8 2.4 %collective-permute-start.1 = (bf16[32,888]{1,0:T(8,128)(2,1)S(1)}, bf16[32,888]{1,0:T(8,128)(2,1)S(1)}, u32[]{:S(2)}, u32[]{:S(2)}) collective-permute-start(bf16[32,888]{1,0:T(8,128)(2,1)S(1)} %get-tuple-element.33), channel_id=1, source_target_pairs={{0,1},{1,0},{2,3},{3,2},{4,5},{5,4},{6,7},{7,6},{8,9},{9,8},{10,11... | collective-permute-start | bytes 170504 | tf_op jit(solution)/shard_map/ppermute | solution.py:68
  34.2 2.8 %collective-permute-done.2 = bf16[32,888]{1,0:T(8,128)(2,1)S(1)} collective-permute-done((bf16[32,888]{1,0:T(8,128)(2,1)S(1)}, bf16[32,888]{1,0:T(8,128)(2,1)S(1)}, u32[]{:S(2)}, u32[]{:S(2)}) %collective-permute-start.2) | collective-permute-done | bytes 56864 | tf_op jit(solution)/shard_map/ppermute | solution.py:68
  37.0 0.9 collective-permute-done.1
  38.5 0.3 copy.37
  38.8 1.3 %broadcast_in_dim.37 = bf16[8,16,16,320]{3,2,1,0:T(8,128)(2,1)} broadcast(bf16[16,16,320]{2,1,0:T(8,128)(2,1)S(1)} %all-to-all-done), dimensions={1,2,3} | broadcast | bytes 1474560 | tf_op jit(solution)/shard_map/broadcast_in_dim | solution.py:17
  40.1 4.2 %all-to-all-start.1 = ((bf16[8,16,16,320]{3,2,1,0:T(8,128)(2,1)}), bf16[8,16,16,320]{3,2,1,0:T(8,128)(2,1)S(1)}, u32[]{:S(2)}, u32[]{:S(2)}) async-start(bf16[8,16,16,320]{3,2,1,0:T(8,128)(2,1)} %broadcast_in_dim.37), calls=%async_computation.1 | async-start | bytes 3145728 | tf_op jit(solution)/shard_map/all_to_all | solution.py:18
  44.2 57.1 %all-gather.2 = f16[13952,128]{1,0:T(8,128)(2,1)S(1)} all-gather(f16[872,128]{1,0:T(8,128)(2,1)S(1)} %copy.37), channel_id=2, replica_groups=mesh['depth'=16,'near'=2,'far'=2,'core'=2,'answer'=4] {'depth'}, dimensions={0}, use_global_device_ids=true | all-gather | bytes 3794944 | tf_op jit(solution)/shard_map/all_gather | solution.py:84
  101.6 1.5 %copy-done.1 = f16[13952,128]{1,0:T(8,128)(2,1)} copy-done((f16[13952,128]{1,0:T(8,128)(2,1)}, f16[13952,128]{1,0:T(8,128)(2,1)S(1)}, u32[]{:S(2)}) %copy-start.1) | copy-done | bytes 3571736
  103.3 4.0 %fusion = f32[320,864,1]{1,0,2:T(8,128)S(1)} fusion(bf16[16,128,320]{2,1,0:T(8,128)(2,1)S(1)} %bitcast.69, f16[16,872,128]{2,1,0:T(8,128)(2,1)} %bitcast.65, f32[16,128]{1,0:T(8,128)S(1)} %fusion.9), kind=kOutput, calls=%fused_computation.1 | convolution fusion | flops 1137770496 | bytes 5963776 | tf_op jit(solution)/shard_map/dot_general | solution.py:98
  107.4 1.0 add_convert_fusion
  108.4 6.9 %all-to-all-start.2 = ((bf16[8,40,864]{2,1,0:T(8,128)(2,1)}), bf16[8,40,864]{2,1,0:T(8,128)(2,1)S(1)}, u32[]{:S(2)}, u32[]{:S(2)}) async-start(bf16[8,40,864]{2,1,0:T(8,128)(2,1)} %bitcast.26), calls=%async_computation.2 | async-start | bytes 1146880 | tf_op jit(solution)/shard_map/all_to_all | solution.py:114
  115.3 1.9 %collective-permute-start.4 = (bf16[160,864]{1,0:T(8,128)(2,1)S(1)}, bf16[160,864]{1,0:T(8,128)(2,1)S(1)}, u32[]{:S(2)}, u32[]{:S(2)}) collective-permute-start(bf16[160,864]{1,0:T(8,128)(2,1)S(1)} %dynamic-slice_convert_fusion), channel_id=1, source_target_pairs={{0,16},{16,0},{1,17},{17,1},{2,18},{18,2},{3,19},{19,3},{4,20},{20... | collective-permute-start | bytes 829448 | tf_op jit(solution)/shard_map/ppermute | solution.py:110
  117.2 5.6 %all-to-all-done.2 = bf16[8,40,864]{2,1,0:T(8,128)(2,1)S(1)} async-done(((bf16[8,40,864]{2,1,0:T(8,128)(2,1)}), bf16[8,40,864]{2,1,0:T(8,128)(2,1)S(1)}, u32[]{:S(2)}, u32[]{:S(2)}) %all-to-all-start.2) | async-done | bytes 552992 | tf_op jit(solution)/shard_map/all_to_all | solution.py:114
  123.0 0.9 reshape.259
  124.0 0.9 convert_add_fusion
  (47 shorter events, 2.2 us)
Async XLA Ops:
  0.6 1.0 copy-start
  0.6 20.8 %copy-start.3 = (bf16[32,3456]{1,0:T(8,128)(2,1)S(1)}, bf16[32,3456]{1,0:T(8,128)(2,1)}, u32[]{:S(2)}) copy-start(bf16[32,3456]{1,0:T(8,128)(2,1)} %param.6) | copy-start | bytes 663556
  3.5 35.3 %all-to-all-start = ((bf16[16,16,320]{2,1,0:T(8,128)(2,1)}), bf16[16,16,320]{2,1,0:T(8,128)(2,1)S(1)}, u32[]{:S(2)}, u32[]{:S(2)}) async-start(bf16[16,16,320]{2,1,0:T(8,128)(2,1)} %copy.34), calls=%async_computation | async-start | bytes 393216 | tf_op jit(solution)/shard_map/all_to_all | solution.py:48
  18.7 5.4 %collective-permute-start = (f32[128]{0:T(128)S(1)}, f32[128]{0:T(128)S(1)}, u32[]{:S(2)}, u32[]{:S(2)}) collective-permute-start(f32[128]{0:T(128)S(1)} %reduce_sum.34), channel_id=1, source_target_pairs={{0,16},{16,0},{1,17},{17,1},{2,18},{18,2},{3,19},{19,3},{4,20},{20... | collective-permute-start | bytes 1544 | tf_op jit(solution)/shard_map/ppermute | solution.py:53
  24.3 9.8 %collective-permute-start.3 = (bf16[32,888]{1,0:T(8,128)(2,1)S(1)}, bf16[32,888]{1,0:T(8,128)(2,1)S(1)}, u32[]{:S(2)}, u32[]{:S(2)}) collective-permute-start(bf16[32,888]{1,0:T(8,128)(2,1)S(1)} %get-tuple-element.35), channel_id=1, source_target_pairs={{0,3},{1,2},{2,1},{3,0},{4,7},{5,6},{6,5},{7,4},{8,11},{9,10},{10,... | collective-permute-start | bytes 170504 | tf_op jit(solution)/shard_map/ppermute | solution.py:68
  29.3 7.7 %collective-permute-start.2 = (bf16[32,888]{1,0:T(8,128)(2,1)S(1)}, bf16[32,888]{1,0:T(8,128)(2,1)S(1)}, u32[]{:S(2)}, u32[]{:S(2)}) collective-permute-start(bf16[32,888]{1,0:T(8,128)(2,1)S(1)} %get-tuple-element.34), channel_id=1, source_target_pairs={{0,2},{1,3},{2,0},{3,1},{4,6},{5,7},{6,4},{7,5},{8,10},{9,11},{10,... | collective-permute-start | bytes 170504 | tf_op jit(solution)/shard_map/ppermute | solution.py:68
  31.8 6.1 %collective-permute-start.1 = (bf16[32,888]{1,0:T(8,128)(2,1)S(1)}, bf16[32,888]{1,0:T(8,128)(2,1)S(1)}, u32[]{:S(2)}, u32[]{:S(2)}) collective-permute-start(bf16[32,888]{1,0:T(8,128)(2,1)S(1)} %get-tuple-element.33), channel_id=1, source_target_pairs={{0,1},{1,0},{2,3},{3,2},{4,5},{5,4},{6,7},{7,6},{8,9},{9,8},{10,11... | collective-permute-start | bytes 170504 | tf_op jit(solution)/shard_map/ppermute | solution.py:68
  40.1 63.0 %all-to-all-start.1 = ((bf16[8,16,16,320]{3,2,1,0:T(8,128)(2,1)}), bf16[8,16,16,320]{3,2,1,0:T(8,128)(2,1)S(1)}, u32[]{:S(2)}, u32[]{:S(2)}) async-start(bf16[8,16,16,320]{3,2,1,0:T(8,128)(2,1)} %broadcast_in_dim.37), calls=%async_computation.1 | async-start | bytes 3145728 | tf_op jit(solution)/shard_map/all_to_all | solution.py:18
  101.3 1.8 %copy-start.1 = (f16[13952,128]{1,0:T(8,128)(2,1)}, f16[13952,128]{1,0:T(8,128)(2,1)S(1)}, u32[]{:S(2)}) copy-start(f16[13952,128]{1,0:T(8,128)(2,1)S(1)} %all-gather.2) | copy-start | bytes 10715140
  103.3 4.0 %copy-start.2 = (f32[160,864]{1,0:T(8,128)S(1)}, f32[160,864]{1,0:T(8,128)}, u32[]{:S(2)}) copy-start(f32[160,864]{1,0:T(8,128)} %param.4) | copy-start | bytes 1658884
  108.4 14.4 %all-to-all-start.2 = ((bf16[8,40,864]{2,1,0:T(8,128)(2,1)}), bf16[8,40,864]{2,1,0:T(8,128)(2,1)S(1)}, u32[]{:S(2)}, u32[]{:S(2)}) async-start(bf16[8,40,864]{2,1,0:T(8,128)(2,1)} %bitcast.26), calls=%async_computation.2 | async-start | bytes 1146880 | tf_op jit(solution)/shard_map/all_to_all | solution.py:114
  115.3 8.7 %collective-permute-start.4 = (bf16[160,864]{1,0:T(8,128)(2,1)S(1)}, bf16[160,864]{1,0:T(8,128)(2,1)S(1)}, u32[]{:S(2)}, u32[]{:S(2)}) collective-permute-start(bf16[160,864]{1,0:T(8,128)(2,1)S(1)} %dynamic-slice_convert_fusion), channel_id=1, source_target_pairs={{0,16},{16,0},{1,17},{17,1},{2,18},{18,2},{3,19},{19,3},{4,20},{20... | collective-permute-start | bytes 829448 | tf_op jit(solution)/shard_map/ppermute | solution.py:110
